TPU v7x, 512 devices: a whole 4x4x16 slice. The times are simulated.
512 devices in a mesh: dp: 128 (over z, x, core), rep: 4 (over y).
Axes of the slice: x: 4, y: 4, z: 16, core: 2. Of those that a mesh axis runs over, the one named last changes fastest.
Arguments:
- gradient: bfloat16 [128, 4, 1024, 1024], P('dp', 'rep'), may hold values from -512 to 512
- owner_list: int32 [256, 1], replicated, may hold values from 0 to 127, as said below
- step_count: int32 [1], replicated, may hold values from 1 to 29
- master: float32 [128, 4, 4096], P('dp', None, 'rep'), may hold values from -3 to 3
- first_moment: float32 [128, 4, 4096], P('dp', None, 'rep'), may hold values from -6 to 6
- second_moment: float32 [128, 4, 4096], P('dp', None, 'rep'), may hold values from 0.25 to 4
Outputs:
- weights: bfloat16 [1024, 1024], replicated
- new_master: float32 [128, 4, 4096], P('dp', None, 'rep')
- new_first: float32 [128, 4, 4096], P('dp', None, 'rep')
- new_second: float32 [128, 4, 4096], P('dp', None, 'rep')
Inputs may be any that keep to these rules, and one draw needn't show every extreme that they name: `owner_list`: every index along dp owns at least one block and at most 4; some index owns exactly 4.
All inputs are finite; a program needn't handle non-finite values.
Results may differ from a plain program's by a relative error of at most 0.0004.
Values may be sent and summed in bfloat16 or wider, within the bound.
A program may use at most 64 MiB of HBM per device.

v0:
```python
import jax
import jax.numpy as jnp
from jax import lax
from jax.sharding import PartitionSpec as P


def local(gradient, owner_list, step_count, master, first_moment, second_moment):
    n_dp = lax.axis_size("dp")
    n_rep = lax.axis_size("rep")
    slot_count = master.shape[1]
    quarter_width = master.shape[2]
    block_width = quarter_width * n_rep
    row_count = gradient.shape[2]
    feature_count = gradient.shape[3]
    block_count = row_count * feature_count // block_width
    blocks = gradient.reshape(block_count, block_width)
    owner_of = owner_list[:, 0]
    block_ids = jnp.arange(block_count, dtype=jnp.int32)
    earlier = (owner_of[:, None] == owner_of[None, :]) & (block_ids[None, :] < block_ids[:, None])
    slot_rank = jnp.sum(earlier.astype(jnp.int32), axis=1)
    position = owner_of * slot_count + slot_rank
    layout_ids = jnp.arange(n_dp * slot_count, dtype=jnp.int32)
    matches = position[None, :] == layout_ids[:, None]
    filled = jnp.any(matches, axis=1)
    picked = jnp.sum(jnp.where(matches, block_ids[None, :], 0), axis=1)
    outgoing = jnp.where(filled[:, None], blocks[picked], jnp.zeros((), gradient.dtype))
    outgoing = outgoing.reshape(n_dp, slot_count, block_width)
    arrived = lax.all_to_all(outgoing, "dp", split_axis=0, concat_axis=0, tiled=True)
    partial_sum = jnp.sum(arrived, axis=0, dtype=jnp.float32)
    owned_sum = lax.psum_scatter(partial_sum, "rep", scatter_dimension=1, tiled=True)
    squares_total = lax.psum(jnp.sum(owned_sum * owned_sum), ("dp", "rep"))
    limit = jnp.sqrt(jnp.float32(row_count * feature_count))
    scale = limit / jnp.maximum(jnp.sqrt(squares_total), limit)
    my_index = lax.axis_index("dp")
    my_filled = lax.dynamic_slice_in_dim(filled.reshape(n_dp, slot_count), my_index, 1, 0)[0][
        :, None
    ]
    clipped = scale * owned_sum
    old_master = master[0]
    old_first = first_moment[0]
    old_second = second_moment[0]
    new_first = jnp.where(my_filled, 0.9 * old_first + 0.1 * clipped, 0.0)
    new_second = jnp.where(my_filled, 0.95 * old_second + 0.05 * clipped * clipped, 0.0)
    step_value = step_count[0].astype(jnp.float32)
    first_fix = 1.0 - jnp.power(jnp.float32(0.9), step_value)
    second_fix = 1.0 - jnp.power(jnp.float32(0.95), step_value)
    update = new_first / first_fix / (jnp.sqrt(new_second / second_fix) + 1e-08)
    new_master = jnp.where(my_filled, old_master * (1.0 - 0.1 * 0.1) - 0.1 * update, 0.0)
    rounded = new_master.astype(jnp.bfloat16)
    joined = lax.all_gather(rounded, "rep", axis=1, tiled=True)
    collected = lax.all_gather(joined[None], "dp", axis=0, tiled=True)
    stacked = collected.reshape(n_dp * slot_count, block_width)
    weights = stacked[position].reshape(row_count, feature_count)
    return (weights, new_master[None], new_first[None], new_second[None])


def solution(mesh):
    placed = (
        P("dp", "rep", None, None),
        P(),
        P(),
        P("dp", None, "rep"),
        P("dp", None, "rep"),
        P("dp", None, "rep"),
    )
    return jax.shard_map(
        local,
        mesh=mesh,
        in_specs=placed,
        out_specs=(P(), P("dp", None, "rep"), P("dp", None, "rep"), P("dp", None, "rep")),
        check_vma=False,
    )
```

profile of v0, /device:TPU:1, one launch (start us, length us, event | category | flops | bytes accessed | tf_op | source)
XLA Modules:
  0.0 552.6 jit_solution(9069480816287428504)
XLA Ops:
  7.2 0.0 reduce-scatter.4.cloned.1.call-start
  7.2 0.9 convert_reduce_fusion.1
  8.1 0.7 multiply_add_fusion
  8.8 0.2 fusion
  9.0 0.2 select_reduce_fusion
  9.1 0.1 reshape.67
  9.3 3.1 reshape.68
  12.4 4.4 gather_fusion
  16.8 7.2 %gather.9 = bf16[128,4,4096]{2,1,0:T(4,128)(2,1)} reshape(bf16[512,4096]{1,0:T(8,128)(2,1)} %gather_fusion) | data formatting | bytes 8388608 | tf_op jit(solution)/shard_map/gather | solution.py:26
  24.0 4.1 broadcast_select_fusion
  28.0 204.1 %all_to_all.5 = bf16[128,4,4096]{2,1,0:T(4,128)(2,1)S(1)} all-to-all(bf16[128,4,4096]{2,1,0:T(4,128)(2,1)S(1)} %broadcast_select_fusion), channel_id=1, replica_groups=mesh['dp'=128,'rep'=4] {'dp'}, dimensions={0} | all-to-all | bytes 8388608 | tf_op jit(solution)/shard_map/all_to_all | solution.py:28
  232.1 0.0 copy-start
  232.1 0.0 copy-start.1
  232.1 0.0 copy-start.2
  232.1 0.0 copy-start.3
  232.1 1.7 convert_reduce_fusion
  233.8 2.0 copy.10
  235.8 0.0 reduce-scatter.4.cloned.1.call-update
  235.8 0.0 all-gather.4.cloned.1.call-start
  236.6 34.8 %reduce-scatter.4.cloned.1.call-done = f32[1024,4]{1,0:T(8,128)} async-done(((f32[4096,4]{1,0:T(8,128)}), f32[1024,4]{1,0:T(8,128)}) %reduce-scatter.4.cloned.1.call-update) | async-done | bytes 16400
  271.4 1.2 copy.11
  272.6 0.6 multiply_reduce_fusion
  273.3 104.2 %psum.7 = f32[]{:T(128)} all-reduce(f32[]{:T(128)} %multiply_reduce_fusion), channel_id=1, replica_groups=mesh['dp'=128,'rep'=4] {'dp','rep'}, use_global_device_ids=true, to_apply=%region_6.7 | all-reduce | flops 1 | bytes 8 | tf_op jit(solution)/shard_map/psum | solution.py:31
  378.2 0.0 copy-done
  378.2 0.0 copy-done.1
  378.2 0.0 copy-done.2
  378.2 0.7 fusion.8
  378.9 10.1 %all_gather.6 = bf16[4,4096]{1,0:T(4,128)(2,1)} all-gather(bf16[4,1024]{1,0:T(4,128)(2,1)S(1)} %get-tuple-element.4), channel_id=1, replica_groups=mesh['dp'=128,'rep'=4] {'rep'}, dimensions={1}, use_global_device_ids=true | all-gather | bytes 40960 | tf_op jit(solution)/shard_map/all_gather | solution.py:50
  389.0 0.0 all-gather.4.cloned.1.call-update
  389.0 0.0 copy-done.3
  389.0 140.6 %all-gather.4.cloned.1.call-done = bf16[128,4,4096]{2,1,0:T(4,128)(2,1)} async-done(((bf16[1,4,4096]{2,1,0:T(4,128)(2,1)}), bf16[128,4,4096]{2,1,0:T(4,128)(2,1)}) %all-gather.4.cloned.1.call-update) | async-done | bytes 4194320 | tf_op jit(solution)/shard_map/all_gather | solution.py:51
  529.6 6.9 %reshape.90 = bf16[512,4096]{1,0:T(8,128)(2,1)} reshape(bf16[128,4,4096]{2,1,0:T(4,128)(2,1)} %all-gather.4.cloned.1.call-done) | data formatting | bytes 8388608
  536.5 6.6 %gather_fusion.1 = bf16[256,4096]{1,0:T(8,128)(2,1)S(1)} fusion(bf16[512,4096]{1,0:T(8,128)(2,1)} %reshape.90, s32[1024]{0:T(1024)S(1)} %pad_clamp_fusion), kind=kCustom, calls=%fused_computation.1 | custom fusion | bytes 4195328 | tf_op jit(solution)/shard_map/gather | solution.py:53
  543.2 2.6 reshape.70
  (5 shorter events, 0.0 us)
Async XLA Ops:
  7.2 264.2 %reduce-scatter.4.cloned.1.call-start = ((), (), s32[]{:S(2)}) async-start(), calls=%async_computation.3 | async-start | bytes 2621440
  232.1 146.1 %copy-start = (f32[1,4,1024]{2,1,0:T(4,128)S(1)}, f32[1,4,1024]{2,1,0:T(4,128)}, u32[]{:S(2)}) copy-start(f32[1,4,1024]{2,1,0:T(4,128)} %param.11) | copy-start | bytes 49156
  232.1 146.1 %copy-start.1 = (f32[1,4,1024]{2,1,0:T(4,128)S(1)}, f32[1,4,1024]{2,1,0:T(4,128)}, u32[]{:S(2)}) copy-start(f32[1,4,1024]{2,1,0:T(4,128)} %param.10) | copy-start | bytes 49156
  232.1 146.1 %copy-start.2 = (f32[1,4,1024]{2,1,0:T(4,128)S(1)}, f32[1,4,1024]{2,1,0:T(4,128)}, u32[]{:S(2)}) copy-start(f32[1,4,1024]{2,1,0:T(4,128)} %param.9) | copy-start | bytes 49156
  232.1 156.9 %copy-start.3 = (s32[256,1]{0,1:T(1,128)S(1)}, s32[256,1]{0,1:T(1,128)}, u32[]{:S(2)}) copy-start(s32[256,1]{0,1:T(1,128)} %param.7) | copy-start | bytes 3076
  235.8 293.8 %all-gather.4.cloned.1.call-start = ((), (), s32[]{:S(2)}) async-start(), calls=%async_computation.2 | async-start | bytes 4227072 | tf_op jit(solution)/shard_map/all_gather | solution.py:51
Sparse Core Ops, SparseCore 0:
  235.9 35.4 reduce-scatter.3
  389.1 140.4 all-gather.3
where the time goes:
time: 553 us
  blocking collectives  318 us (58%)
  waiting for transfers between devices  175 us (32%)
  local copies, waits for them, and re-layouts  34.1 us (6%)
  between operations  15.6 us (3%)
  other arithmetic  9.06 us (2%)
    all_to_all x1, blocking collectives, local(): lax.all_to_all(outgoing, 'dp', split_axis=0, concat_axis=0, tiled=True)  204 us
    all_gather x1, waiting for transfers between devices, local(): collected = lax.all_gather(joined[None], 'dp', axis=0, tiled=True)  141 us
    psum x1, blocking collectives, local(): squares_total = lax.psum(jnp.sum(owned_sum * owned_sum), ('dp', 'rep'))  104 us
    unnamed x3, waiting for transfers between devices  34.8 us
    gather x2, local copies, waits for them, and re-layouts, local(): blocks[picked]  11.5 us
  transfers between devices with their start and end apart: 2, of which 2 were waited for; matrix products, arithmetic and copies ran while one was open for 0% of the time, Pallas kernels for 0%

commit v1 on v0

v1 whole, which is shorter than its diff:
```python
import functools

import jax
import jax.numpy as jnp
from jax import lax
from jax.experimental import pallas as pl
from jax.experimental.pallas import tpu as pltpu
from jax.sharding import PartitionSpec as P

MESH = pl.DeviceIdType.MESH
F32 = jnp.float32
BF16 = jnp.bfloat16
HIGH = lax.Precision.HIGHEST
NZ = 16
NFLOW = 4
NSEM = 256


def flip1(v):
    return v + 1 - 2 * (v % 2)


def flip2(v):
    return (v + 2) % 4


def flip3(v):
    return 3 - v


def integer_power(base, count):
    result = jnp.ones((1, 1), F32)
    factor = jnp.float32(base)
    for bit in range(5):
        result = jnp.where((count // (2**bit)) % 2 == 1, result * factor, result)
        factor = factor * factor
    return result


def adam(total, master, first, second, scale, first_fix, second_fix):
    clipped = scale * total
    new_first = 0.9 * first + 0.1 * clipped
    new_second = 0.95 * second + 0.05 * clipped * clipped
    update = new_first / first_fix / (jnp.sqrt(new_second / second_fix) + 1e-08)
    new_master = master * (1.0 - 0.1 * 0.1) - 0.1 * update
    return new_master, new_first, new_second


def kernel(
    grad,
    owner_ref,
    step_ref,
    master_ref,
    first_ref,
    second_ref,
    w_out,
    nm_out,
    nf_out,
    ns_out,
    own_half,
    core_in,
    rows_f32,
    part,
    in1,
    in2,
    in3,
    in4,
    zsend,
    zin,
    sums,
    squares,
    sel_out,
    sel_in,
    opt_out,
    opt_in,
    opt_all,
    onehot,
    w_part,
    w_rows,
    local_sem,
    send_sem,
    recv_sem,
):
    d = lax.axis_index("dp")
    y = lax.axis_index("rep")
    z = d // 8
    w = d % 8
    x = w // 2
    c = d % 2
    slab = c * 4 + x

    def dev(zz, xx, cc, yy):
        return (zz * 8 + xx * 2 + cc, yy)

    counter = [0]

    def remote(src, dst, device):
        i = counter[0]
        counter[0] += 1
        return pltpu.make_async_remote_copy(
            src_ref=src,
            dst_ref=dst,
            send_sem=send_sem.at[i],
            recv_sem=recv_sem.at[i],
            device_id=device,
            device_id_type=MESH,
        )

    sent = []

    def start(copy):
        copy.start()
        sent.append(copy)
        return copy

    partner = dev(z, x, 1 - c, y)

    local = []
    for f in range(NFLOW):
        local.append(
            pltpu.make_async_copy(
                grad.at[pl.ds(256 * f, 256), pl.ds(pl.multiple_of(512 * c, 512), 512)],
                own_half.at[f],
                local_sem.at[f],
            )
        )
        local[f].start()

    barrier = pltpu.get_barrier_semaphore()
    q = (y * 4 + x) * 2 + c

    def slab_peer(o):
        p = (q + o) % 32
        return dev(z, (p // 2) % 4, p % 2, p // 8)

    for o in range(1, 32):
        pl.semaphore_signal(barrier, inc=1, device_id=slab_peer(o), device_id_type=MESH)
    for o in range(1, NZ):
        pl.semaphore_signal(
            barrier, inc=1, device_id=dev((z + o) % NZ, x, c, y), device_id_type=MESH
        )
    pl.semaphore_wait(barrier, 31 + NZ - 1)

    core_copies = []
    for f in range(NFLOW):
        core_copies.append(
            start(
                remote(
                    grad.at[
                        pl.ds(256 * f, 256), pl.ds(pl.multiple_of(512 * (1 - c), 512), 512)
                    ],
                    core_in.at[f],
                    partner,
                )
            )
        )

    def opt_cols(k):
        return (
            master_ref[0, :, 128 * k : 128 * k + 128],
            first_ref[0, :, 128 * k : 128 * k + 128],
            second_ref[0, :, 128 * k : 128 * k + 128],
        )

    for k in range(8):
        for a, piece in enumerate(opt_cols(k)):
            opt_out[k, a] = piece
    opt_copies = []
    for o in range(1, 8):
        wt = (w + o) % 8
        xt = wt // 2
        ct = wt % 2
        opt_copies.append(
            start(remote(opt_out.at[ct * 4 + xt], opt_in.at[o], dev(z, xt, ct, y)))
        )
    opt_in[0] = opt_out[slab]

    flows = []
    for f in range(NFLOW):
        along_x = f % 2 == 0
        s0, s1 = (flip1, flip3) if f < 2 else (flip3, flip1)
        c1, c2 = (x, y) if along_x else (y, x)
        peer_x = lambda v: dev(z, v, c, y)
        peer_y = lambda v: dev(z, x, c, v)
        peer1, peer2 = (peer_x, peer_y) if along_x else (peer_y, peer_x)
        flows.append((along_x, s0, s1, c1, c2, peer1, peer2))

    step1 = []
    for f in range(NFLOW):
        along_x, s0, s1, c1, c2, peer1, peer2 = flows[f]
        local[f].wait()
        core_copies[f].wait_recv()
        for kx in range(4):
            cols = slice(128 * kx, 128 * kx + 128)
            rows_f32[kx] = own_half[f, :, cols].astype(F32) + core_in[f, :, cols].astype(F32)
            for r in range(4):
                i, j = (kx, r) if along_x else (r, kx)
                part[f, i, j] = rows_f32[kx, pl.ds(r, 64, stride=4), :]
        p = s0(c1)
        a = start(remote(part.at[f, flip2(c1)], in1.at[f, 0], peer1(p)))
        b = start(remote(part.at[f, p], in1.at[f, 1], peer1(p)))
        step1.append((a, b))

    for o in range(1, 8):
        opt_copies[o - 1].wait_recv()
    for o in range(8):
        ws = (w + 8 - o) % 8
        for a in range(3):
            opt_all[z, a, pl.ds(ws * 4, 4), :] = opt_in[o, a]
    ring_r = []
    ring_l = []

    def ring_step(s):
        if s > 1:
            ring_r[s - 2].wait_recv()
            if s - 2 < len(ring_l):
                ring_l[s - 2].wait_recv()
        if s <= 8:
            at = (z + NZ - s + 1) % NZ
            ring_r.append(start(remote(opt_all.at[at], opt_all.at[at], dev((z + 1) % NZ, x, c, y))))
        if s <= 7:
            at = (z + s - 1) % NZ
            ring_l.append(
                start(remote(opt_all.at[at], opt_all.at[at], dev((z + NZ - 1) % NZ, x, c, y)))
            )

    ring_step(1)

    owner_col = jnp.broadcast_to(owner_ref[...], (256, 256))
    row_id = lax.broadcasted_iota(jnp.int32, (256, 256), 0)
    col_id = lax.broadcasted_iota(jnp.int32, (256, 256), 1)
    owner_row = jnp.sum(jnp.where(row_id == col_id, owner_col, 0), axis=0, keepdims=True)
    same = owner_col == owner_row
    rank_col = jnp.sum(
        jnp.where(same & (col_id < row_id), 1.0, 0.0), axis=1, keepdims=True
    ).astype(jnp.int32)
    rank_row = jnp.sum(jnp.where(same & (row_id < col_id), 1, 0), axis=0, keepdims=True)
    pos_col = owner_ref[...] * 4 + rank_col
    pos_row = owner_row * 4 + rank_row
    onehot[...] = (pos_col == lax.broadcasted_iota(jnp.int32, (256, 512), 1)).astype(F32)
    chosen = (
        pos_row == z * 32 + lax.broadcasted_iota(jnp.int32, (32, 256), 0)
    ).astype(F32)
    mine = (pos_row == d * 4 + lax.broadcasted_iota(jnp.int32, (4, 256), 0)).astype(F32)
    filled = jnp.sum(mine, axis=1, keepdims=True) > 0.5

    step2 = []
    for f in range(NFLOW):
        along_x, s0, s1, c1, c2, peer1, peer2 = flows[f]
        qq = s1(c1)
        step1[f][0].wait_recv()
        part[f, qq] = part[f, qq] + in1[f, 0]
        step2.append(start(remote(part.at[f, qq], in2.at[f], peer1(qq))))
    ring_step(2)
    step3 = []
    for f in range(NFLOW):
        along_x, s0, s1, c1, c2, peer1, peer2 = flows[f]
        p = s0(c2)
        step1[f][1].wait_recv()
        step2[f].wait_recv()
        part[f, c1] = part[f, c1] + in1[f, 1] + in2[f]
        a = start(remote(part.at[f, c1, flip2(c2)], in3.at[f, 0], peer2(p)))
        b = start(remote(part.at[f, c1, p], in3.at[f, 1], peer2(p)))
        step3.append((a, b))
        if f % 2 == 1:
            ring_step(3 + f // 2)
    step4 = []
    for f in range(NFLOW):
        along_x, s0, s1, c1, c2, peer1, peer2 = flows[f]
        qq = s1(c2)
        step3[f][0].wait_recv()
        part[f, c1, qq] = part[f, c1, qq] + in3[f, 0]
        step4.append(start(remote(part.at[f, c1, qq], in4.at[f], peer2(qq))))
    ring_step(5)
    for f in range(NFLOW):
        along_x, s0, s1, c1, c2, peer1, peer2 = flows[f]
        step3[f][1].wait_recv()
        step4[f].wait_recv()
        total = part[f, c1, c2] + in3[f, 1] + in4[f]
        for k in range(4):
            zsend[4 * f + k] = total[16 * k : 16 * k + 16]

    order = [8, 7, 9, 6, 10, 5, 11, 4, 12, 3, 13, 2, 14, 1, 15]
    zcopies = []
    for o in order:
        to = (z + o) % NZ
        zcopies.append(start(remote(zsend.at[to], zin.at[o], dev(to, x, c, y))))
    ring_step(6)
    ring_step(7)
    ring_step(8)
    for copy in zcopies:
        copy.wait_recv()
    zin[0] = zsend[z]
    sums[z] = jnp.sum(zin[...], axis=0)
    gathers = []
    for o in order:
        to = (z + o) % NZ
        gathers.append(start(remote(sums.at[z], sums.at[z], dev(to, x, c, y))))
    ring_step(9)
    states = []
    for a in range(3):
        table = opt_all[:, a].reshape(512, 128)
        states.append(jnp.dot(onehot[...], table, precision=HIGH, preferred_element_type=F32))
    for copy in gathers:
        copy.wait_recv()

    summed = sums[...].reshape(256, 128)
    squares[q] = jnp.sum((summed * summed).reshape(32, 8, 128), axis=0)
    norms = []
    for o in range(1, 32):
        norms.append(start(remote(squares.at[q], squares.at[q], slab_peer(o))))
    picked = jnp.dot(chosen, summed, precision=HIGH, preferred_element_type=F32)
    for k in range(8):
        sel_out[k] = picked[4 * k : 4 * k + 4]
    sel_copies = []
    for o in range(1, 8):
        wt = (w + o) % 8
        sel_copies.append(
            start(remote(sel_out.at[wt], sel_in.at[slab], dev(z, wt // 2, wt % 2, y)))
        )
    sel_in[slab] = sel_out[w]

    count = jnp.full((1, 1), step_ref[0], jnp.int32)
    first_fix = 1.0 - integer_power(0.9, count)
    second_fix = 1.0 - integer_power(0.95, count)
    for copy in norms:
        copy.wait_recv()
    squares_total = jnp.sum(jnp.sum(squares[...], axis=0), keepdims=True)
    limit = jnp.float32(1024.0)
    scale = limit / jnp.maximum(jnp.sqrt(squares_total), limit)
    new_slab, _, _ = adam(summed, *states, scale, first_fix, second_fix)
    rounded = new_slab.astype(BF16)

    ag = []
    for f in range(NFLOW):
        along_x, s0, s1, c1, c2, peer1, peer2 = flows[f]
        w_part[c, f, c1, c2] = rounded[64 * f : 64 * f + 64]
        p, qq = s0(c2), s1(c2)
        own = w_part.at[c, f, c1, c2]
        a = start(remote(own, own, peer2(qq)))
        b = start(remote(own, own, peer2(p)))
        ag.append((a, b))
    third = []
    for f in range(NFLOW):
        along_x, s0, s1, c1, c2, peer1, peer2 = flows[f]
        p, qq = s0(c2), s1(c2)
        ag[f][0].wait_recv()
        got = w_part.at[c, f, c1, qq]
        third.append(start(remote(got, got, peer2(p))))

    core_w = []

    def to_partner(piece):
        core_w.append(start(remote(piece, piece, partner)))

    wide = []
    for f in range(NFLOW):
        along_x, s0, s1, c1, c2, peer1, peer2 = flows[f]
        p, qq = s0(c1), s1(c1)
        ag[f][1].wait_recv()
        third[f].wait_recv()
        own = w_part.at[c, f, c1]
        a = start(remote(own, own, peer1(qq)))
        b = start(remote(own, own, peer1(p)))
        wide.append((a, b))
        to_partner(own)

    for copy in sel_copies:
        copy.wait_recv()
    for k in range(8):
        cols = slice(128 * k, 128 * k + 128)
        parts = adam(sel_in[k], *opt_cols(k), scale, first_fix, second_fix)
        for out, value in zip((nm_out, nf_out, ns_out), parts):
            out[0, :, cols] = jnp.where(filled, value, 0.0)

    last = []
    for f in range(NFLOW):
        along_x, s0, s1, c1, c2, peer1, peer2 = flows[f]
        p, qq = s0(c1), s1(c1)
        wide[f][0].wait_recv()
        got = w_part.at[c, f, qq]
        last.append(start(remote(got, got, peer1(p))))
        to_partner(got)
    for f in range(NFLOW):
        along_x, s0, s1, c1, c2, peer1, peer2 = flows[f]
        wide[f][1].wait_recv()
        to_partner(w_part.at[c, f, s0(c1)])
        last[f].wait_recv()
        to_partner(w_part.at[c, f, flip2(c1)])

    def assemble(f, kx, half):
        along_x = flows[f][0]
        for r in range(4):
            i, j = (kx, r) if along_x else (r, kx)
            w_rows[kx, pl.ds(r, 64, stride=4), :] = w_part[half, f, i, j].astype(F32)
        at = pl.multiple_of(512 * half + 128 * kx, 128)
        w_out[pl.ds(256 * f, 256), pl.ds(at, 128)] = w_rows[kx].astype(BF16)

    for f in range(NFLOW):
        for kx in range(4):
            assemble(f, kx, c)
    for copy in core_w:
        copy.wait_recv()
    for f in range(NFLOW):
        for kx in range(4):
            assemble(f, kx, 1 - c)
    for copy in sent:
        copy.wait_send()


def local_step(gradient, owner_list, step_count, master, first_moment, second_moment):
    vmem = pl.BlockSpec(memory_space=pltpu.VMEM)
    state = jax.ShapeDtypeStruct(master.shape, F32)
    return pl.pallas_call(
        kernel,
        out_shape=(jax.ShapeDtypeStruct((1024, 1024), BF16), state, state, state),
        in_specs=[
            pl.BlockSpec(memory_space=pl.ANY),
            vmem,
            pl.BlockSpec(memory_space=pltpu.SMEM),
            vmem,
            vmem,
            vmem,
        ],
        out_specs=(vmem, vmem, vmem, vmem),
        scratch_shapes=[
            pltpu.VMEM((NFLOW, 256, 512), BF16),
            pltpu.VMEM((NFLOW, 256, 512), BF16),
            pltpu.VMEM((4, 256, 128), F32),
            pltpu.VMEM((NFLOW, 4, 4, 64, 128), F32),
            pltpu.VMEM((NFLOW, 2, 4, 64, 128), F32),
            pltpu.VMEM((NFLOW, 4, 64, 128), F32),
            pltpu.VMEM((NFLOW, 2, 64, 128), F32),
            pltpu.VMEM((NFLOW, 64, 128), F32),
            pltpu.VMEM((NZ, 16, 128), F32),
            pltpu.VMEM((NZ, 16, 128), F32),
            pltpu.VMEM((NZ, 16, 128), F32),
            pltpu.VMEM((32, 8, 128), F32),
            pltpu.VMEM((8, 4, 128), F32),
            pltpu.VMEM((8, 4, 128), F32),
            pltpu.VMEM((8, 3, 4, 128), F32),
            pltpu.VMEM((8, 3, 4, 128), F32),
            pltpu.VMEM((NZ, 3, 32, 128), F32),
            pltpu.VMEM((256, 512), F32),
            pltpu.VMEM((2, NFLOW, 4, 4, 64, 128), BF16),
            pltpu.VMEM((4, 256, 128), F32),
            pltpu.SemaphoreType.DMA((NFLOW,)),
            pltpu.SemaphoreType.DMA((NSEM,)),
            pltpu.SemaphoreType.DMA((NSEM,)),
        ],
        compiler_params=pltpu.CompilerParams(collective_id=0, has_side_effects=True),
        name="adam_step",
    )(
        gradient.reshape(gradient.shape[2:]),
        owner_list,
        step_count,
        master,
        first_moment,
        second_moment,
    )


def solution(mesh):
    owned = P("dp", None, "rep")
    return jax.shard_map(
        local_step,
        mesh=mesh,
        in_specs=(P("dp", "rep", None, None), P(), P(), owned, owned, owned),
        out_specs=(P(), owned, owned, owned),
        check_vma=False,
    )
```

time: 553 us -> 97.7 us (0.18)
  blocking collectives: 318 us -> 0 us
  waiting for transfers between devices: 175 us -> 0 us
  Pallas kernels: 0 us -> 89.8 us
  local copies, waits for them, and re-layouts: 34.1 us -> 6.4 us
  between operations: 15.6 us -> 1.31 us
  other arithmetic: 9.06 us -> 0 us
    all_to_all x1 -> x0, blocking collectives: 204 us -> none  [local(): lax.all_to_all(outgoing, 'dp', split_axis=0, concat_axis=0, tiled=True)]
    all_gather x1 -> x0, waiting for transfers between devices: 141 us -> none  [local(): collected = lax.all_gather(joined[None], 'dp', axis=0, tiled=True)]
    psum x1 -> x0, blocking collectives: 104 us -> none  [local(): squares_total = lax.psum(jnp.sum(owned_sum * owned_sum), ('dp', 'rep'))]
    pallas_call x0 -> x1, Pallas kernels: none -> 89.8 us  [local_step(): pl.pallas_call(kernel, out_shape=(jax.ShapeDtypeStruct((1024, 1024), BF16...]
    unnamed x3 -> x0, waiting for transfers between devices: 34.8 us -> none
    gather x3 -> x0, local copies, waits for them, and re-layouts: 18.2 us -> none  [the longest x2 11.5 us: local(): blocks[picked]]
    all_gather x1 -> x0, blocking collectives: 10.1 us -> none  [local(): joined = lax.all_gather(rounded, 'rep', axis=1, tiled=True)]
    reshape x3 -> x0, local copies, waits for them, and re-layouts: 5.79 us -> none  [the longest x1 3.1 us: local(): blocks = gradient.reshape(block_count, block_width)]
  transfers between devices with their start and end apart: 2 -> 0, of which waited for: 2 -> 0; matrix products, arithmetic and copies ran while one was open for 0% -> 0% of each run, Pallas kernels for 0% -> 0%
where the time goes in v1:
time: 97.7 us; the launch traced here: 97.5 us
  Pallas kernels  89.8 us (92%)
  local copies, waits for them, and re-layouts  6.4 us (7%)
  between operations  1.31 us (1%)
    pallas_call x1, Pallas kernels, local_step(): pl.pallas_call(kernel, out_shape=(jax.ShapeDtypeStruct((1024, 1024), BF16...  89.8 us
    unnamed x11, local copies, waits for them, and re-layouts  6.4 us

profile of v1, /device:TPU:1, one launch (start us, length us, event | category | flops | bytes accessed | tf_op | source)
XLA Modules:
  0.0 97.5 jit_solution(8801667073476401809)
XLA Ops:
  1.3 1.5 %copy.10.owner_ref = s32[256,1]{1,0:T(8,128)} copy(s32[256,1]{0,1:T(1,128)} %param.7) | data formatting | bytes 2048 | tf_op args[1]
  2.8 89.8 %adam_step.1 = (bf16[1024,1024]{1,0:T(8,128)(2,1)}, f32[1,4,1024]{2,1,0:T(4,128)}, f32[1,4,1024]{2,1,0:T(4,128)}, f32[1,4,1024]{2,1,0:T(4,128)}) custom-call(bf16[1024,1024]{1,0:T(8,128)(2,1)} %bitcast.1, s32[256,1]{1,0:T(8,128)} %copy.10.owner_ref, s32[1]{0:T(128)S(6)} %copy.15.step_ref, f32[1,4,1024]{2,1,0:T(4,128)} %master_ref.1, ...), custom_call_target="tpu_custom_call" | custom-call | tf_op jit(solution)/shard_map/adam_step/pallas_call | solution.py:414
  92.6 0.0 copy-start.2
  92.6 0.0 copy-start.1
  92.6 0.0 copy-start
  92.6 3.1 %copy.16 = bf16[1024,1024]{1,0:T(8,128)(2,1)} copy(bf16[1024,1024]{1,0:T(8,128)(2,1)} %get-tuple-element.8) | data formatting | bytes 4194304
  95.7 0.0 copy-done.2
  95.7 0.6 copy.17
  96.3 0.0 copy-done.1
  96.3 0.6 copy.18
  96.9 0.0 copy-done
  96.9 0.6 copy.19
Async XLA Ops:
  92.6 3.1 %copy-start.2 = (f32[1,4,1024]{2,1,0:T(4,128)S(1)}, f32[1,4,1024]{2,1,0:T(4,128)}, u32[]{:S(2)}) copy-start(f32[1,4,1024]{2,1,0:T(4,128)} %get-tuple-element.9) | copy-start | bytes 49156
  92.6 3.7 %copy-start.1 = (f32[1,4,1024]{2,1,0:T(4,128)S(1)}, f32[1,4,1024]{2,1,0:T(4,128)}, u32[]{:S(2)}) copy-start(f32[1,4,1024]{2,1,0:T(4,128)} %get-tuple-element.10) | copy-start | bytes 49156
  92.6 4.3 %copy-start = (f32[1,4,1024]{2,1,0:T(4,128)S(1)}, f32[1,4,1024]{2,1,0:T(4,128)}, u32[]{:S(2)}) copy-start(f32[1,4,1024]{2,1,0:T(4,128)} %get-tuple-element.11) | copy-start | bytes 49156

commit v2 on v0

v2 whole, which is shorter than its diff:
```python
import jax
import jax.numpy as jnp
from jax import lax
from jax.experimental import pallas as pl
from jax.experimental.pallas import tpu as pltpu
from jax.sharding import PartitionSpec as P

MESH = pl.DeviceIdType.MESH
F32 = jnp.float32
BF16 = jnp.bfloat16
HIGH = lax.Precision.HIGHEST
NZ = 16
FLOWS = (0, 2, 1, 3)


def flip1(v):
    return v + 1 - 2 * (v % 2)


def flip2(v):
    return (v + 2) % 4


def flip3(v):
    return 3 - v


def integer_power(base, count):
    result = jnp.ones((1, 1), F32)
    factor = jnp.float32(base)
    for bit in range(5):
        result = jnp.where((count // (2**bit)) % 2 == 1, result * factor, result)
        factor = factor * factor
    return result


def corrections(step_ref):
    count = jnp.full((1, 1), step_ref[0], jnp.int32)
    return 1.0 - integer_power(0.9, count), 1.0 - integer_power(0.95, count)


def adam(total, master, first, second, scale, first_fix, second_fix):
    clipped = scale * total
    new_first = 0.9 * first + 0.1 * clipped
    new_second = 0.95 * second + 0.05 * clipped * clipped
    update = new_first / first_fix / (jnp.sqrt(new_second / second_fix) + 1e-08)
    new_master = master * (1.0 - 0.1 * 0.1) - 0.1 * update
    return new_master, new_first, new_second


def reduce_kernel(
    grad,
    owner_ref,
    step_ref,
    master_ref,
    first_ref,
    second_ref,
    w_all,
    small,
    g,
    gy,
    tmp,
    in1x,
    in1y,
    core_out,
    core_in,
    part,
    in2,
    in3,
    zsend,
    zin,
    sums,
    sq1,
    sq2,
    sel_out,
    opt_out,
    opt_in,
    opt_all,
    onehot,
    w_part,
    load_sem,
    step1_sem,
    core_sem,
    step2_sem,
    dim2_sem,
    opt_sem,
    ring_sem,
    z_sem,
    norm_sem,
    ag2_sem,
    ag1_sem,
    out_sem,
    send_sem,
):
    d = lax.axis_index("dp")
    y = lax.axis_index("rep")
    z = d // 8
    w = d % 8
    x = w // 2
    c = d % 2
    slab = c * 4 + x

    def dev(zz, xx, cc, yy):
        return (zz * 8 + xx * 2 + cc, yy)

    def remote(src, dst, send, recv, device):
        copy = pltpu.make_async_remote_copy(
            src_ref=src,
            dst_ref=dst,
            send_sem=send,
            recv_sem=recv,
            device_id=device,
            device_id_type=MESH,
        )
        copy.start()
        return copy

    def drain(ref, sem):
        pltpu.make_async_copy(ref, ref, sem).wait()

    partner = dev(z, x, 1 - c, y)

    loads = {}
    for f in (1, 3, 0, 2):
        loads[f] = pltpu.make_async_copy(
            grad.at[pl.ds(256 * f, 256)], g.at[pl.ds(256 * f, 256)], load_sem.at[f]
        )
        loads[f].start()

    def xc_peer(o):
        t = (w + o) % 8
        return dev(z, t // 2, t % 2, y)

    right = dev((z + 1) % NZ, x, c, y)
    left = dev((z + NZ - 1) % NZ, x, c, y)

    barrier = pltpu.get_barrier_semaphore()
    near = [xc_peer(o) for o in range(1, 8)]
    near += [dev(z, x, c, (y + o) % 4) for o in range(1, 4)] + [right, left]
    for device in near:
        pl.semaphore_signal(barrier, inc=1, device_id=device, device_id_type=MESH)

    states_in = (master_ref, first_ref, second_ref)
    for k in range(8):
        for a in range(3):
            opt_out[k, a] = states_in[a][0, :, 128 * k : 128 * k + 128]

    pl.semaphore_wait(barrier, len(near))

    for o in range(1, 8):
        t = (w + o) % 8
        remote(
            opt_out.at[(t % 2) * 4 + t // 2], opt_in.at[o], send_sem.at[0], opt_sem.at[0], xc_peer(o)
        )
    opt_in[0] = opt_out[slab]

    flows = []
    for f in range(4):
        along_x = f % 2 == 0
        s0, s1 = (flip1, flip3) if f < 2 else (flip3, flip1)
        c1, c2 = (x, y) if along_x else (y, x)
        peer_x = lambda v: dev(z, v, c, y)
        peer_y = lambda v: dev(z, x, c, v)
        peer1, peer2 = (peer_x, peer_y) if along_x else (peer_y, peer_x)
        flows.append((along_x, s0(c1), s1(c1), c1, c2, peer1, peer2))

    def column(core, k):
        return pl.ds(pl.multiple_of(512 * core + 128 * k, 128), 128)

    step1 = {}

    def send_step1(f):
        along_x, p, qq, c1, c2, peer1, peer2 = flows[f]
        h = f // 2
        for k in range(4):
            index = flip2(c1) if k < 2 else p
            core = 1 - c if k % 2 == 0 else c
            if along_x:
                src = grad.at[pl.ds(256 * f, 256), column(core, index)]
                dst = in1x.at[h, k]
            else:
                src = gy.at[h, index, core]
                dst = in1y.at[h, k]
            step1[f, k] = remote(
                src, dst, send_sem.at[1 if along_x else 2], step1_sem.at[f, k], peer1(p)
            )

    send_step1(0)
    send_step1(2)
    for f in (1, 3):
        loads[f].wait()
        for k in range(8):
            tmp[k % 2] = g[256 * f : 256 * f + 256, 128 * k : 128 * k + 128].astype(F32)
            for r in range(4):
                gy[f // 2, r, k // 4, k % 4] = tmp[k % 2, pl.ds(r, 64, stride=4), :].astype(BF16)
        send_step1(f)

    drain(opt_in.at[pl.ds(1, 7)], opt_sem.at[0])
    for o in range(8):
        ws = (w + 8 - o) % 8
        for a in range(3):
            opt_all[z, a, pl.ds(ws * 4, 4), :] = opt_in[o, a]
    ring_r = []
    ring_l = []

    def ring_step():
        s = len(ring_r) + 1
        if s > 9:
            return
        if s > 1:
            ring_r[s - 2].wait_recv()
            if s - 2 < 7:
                ring_l[s - 2].wait_recv()
        if s <= 8:
            at = opt_all.at[(z + NZ - s + 1) % NZ]
            ring_r.append(remote(at, at, send_sem.at[3], ring_sem.at[0, s - 1], right))
        else:
            ring_r.append(None)
        if s <= 7:
            at = opt_all.at[(z + s - 1) % NZ]
            ring_l.append(remote(at, at, send_sem.at[3], ring_sem.at[1, s - 1], left))

    ring_step()
    loads[0].wait()
    loads[2].wait()

    def pair_sum(f, k, put):
        along_x, p, qq, c1, c2, peer1, peer2 = flows[f]
        h = f // 2
        index = qq if k < 2 else c1
        core = 1 - c if k % 2 == 0 else c
        step1[f, k].wait_recv()
        if along_x:
            own = g[256 * f : 256 * f + 256, column(core, index)]
            tmp[h] = own.astype(F32) + in1x[h, k].astype(F32)
            for r in range(4):
                put(r, tmp[h, pl.ds(r, 64, stride=4), :])
        else:
            for j in range(4):
                put(j, gy[h, index, core, j].astype(F32) + in1y[h, k, j].astype(F32))

    core = {}

    def to_core(f, half):
        def put(j, value):
            core_out[f, half, j] = value

        pair_sum(f, 2 * half, put)
        core[f, half] = remote(
            core_out.at[f, half],
            core_in.at[f, half],
            send_sem.at[4],
            core_sem.at[f, half],
            partner,
        )

    def keep(f, half):
        index = flows[f][2] if half == 0 else flows[f][3]

        def put(j, value):
            part[f, index, j] = value

        pair_sum(f, 2 * half + 1, put)

    step2 = {}
    for f in FLOWS:
        to_core(f, 0)
    for f in FLOWS:
        keep(f, 0)
    ring_step()
    for f in FLOWS:
        along_x, p, qq, c1, c2, peer1, peer2 = flows[f]
        core[f, 0].wait_recv()
        part[f, qq] = part[f, qq] + core_in[f, 0]
        step2[f] = remote(
            part.at[f, qq], in2.at[f], send_sem.at[5], step2_sem.at[f], peer1(qq)
        )
    for f in FLOWS:
        to_core(f, 1)
    ring_step()

    row_id = lax.broadcasted_iota(jnp.int32, (256, 256), 0)
    col_id = lax.broadcasted_iota(jnp.int32, (256, 256), 1)
    owner_row = jnp.broadcast_to(owner_ref[...].astype(F32), (256, 256))
    owner_col = jnp.sum(jnp.where(row_id == col_id, owner_row, 0.0), axis=1, keepdims=True)
    same = owner_col == owner_row
    rank_col = jnp.sum(jnp.where(same & (col_id < row_id), 1.0, 0.0), axis=1, keepdims=True)
    rank_row = jnp.sum(jnp.where(same & (row_id < col_id), 1.0, 0.0), axis=0, keepdims=True)
    pos_col = (owner_col * 4.0 + rank_col).astype(jnp.int32)
    pos_row = (owner_ref[...].astype(F32) * 4.0 + rank_row).astype(jnp.int32)
    onehot[...] = (pos_col == lax.broadcasted_iota(jnp.int32, (256, 512), 1)).astype(F32)
    chosen = (pos_row == z * 32 + lax.broadcasted_iota(jnp.int32, (32, 256), 0)).astype(F32)
    mine = (pos_row == d * 4 + lax.broadcasted_iota(jnp.int32, (4, 256), 0)).astype(F32)
    small[9] = jnp.broadcast_to(jnp.sum(mine, axis=1, keepdims=True), (4, 128))

    for f in FLOWS:
        keep(f, 1)
    ring_step()
    for f in FLOWS:
        along_x, p, qq, c1, c2, peer1, peer2 = flows[f]
        core[f, 1].wait_recv()
        step2[f].wait_recv()
        part[f, c1] = part[f, c1] + core_in[f, 1] + in2[f]
        for o in (2, 1, 3):
            to = (c2 + o) % 4
            remote(
                part.at[f, c1, to], in3.at[f, o - 1], send_sem.at[6], dim2_sem.at[f], peer2(to)
            )
    ring_step()
    ring_step()
    for f in FLOWS:
        along_x, p, qq, c1, c2, peer1, peer2 = flows[f]
        drain(in3.at[f], dim2_sem.at[f])
        total = part[f, c1, c2] + in3[f, 0] + in3[f, 1] + in3[f, 2]
        for k in range(4):
            zsend[4 * f + k] = total[16 * k : 16 * k + 16]
    ring_step()
    ring_step()
    ring_step()

    order = [8, 7, 9, 6, 10, 5, 11, 4, 12, 3, 13, 2, 14, 1, 15]
    for o in order:
        to = (z + o) % NZ
        remote(zsend.at[to], zin.at[o], send_sem.at[7], z_sem.at[0], dev(to, x, c, y))
    zin[0] = zsend[z]
    states = []
    for a in range(3):
        table = opt_all[:, a].reshape(512, 128)
        states.append(jnp.dot(onehot[...], table, precision=HIGH, preferred_element_type=F32))
    first_fix, second_fix = corrections(step_ref)
    drain(zin.at[pl.ds(1, 15)], z_sem.at[0])
    sums[z] = jnp.sum(zin[...], axis=0)
    for o in order:
        to = (z + o) % NZ
        remote(sums.at[z], sums.at[z], send_sem.at[8], z_sem.at[1], dev(to, x, c, y))
    drain(sums.at[pl.ds(0, 15)], z_sem.at[1])

    summed = sums[...].reshape(256, 128)
    sq1[w] = jnp.sum((summed * summed).reshape(32, 8, 128), axis=0)
    for o in range(1, 8):
        remote(sq1.at[w], sq1.at[w], send_sem.at[9], norm_sem.at[0], xc_peer(o))
    picked = jnp.dot(chosen, summed, precision=HIGH, preferred_element_type=F32)
    for k in range(8):
        sel_out[k] = picked[4 * k : 4 * k + 4]
    drain(sq1.at[pl.ds(0, 7)], norm_sem.at[0])
    sq2[y] = jnp.sum(sq1[...], axis=0)
    for o in (2, 1, 3):
        remote(sq2.at[y], sq2.at[y], send_sem.at[10], norm_sem.at[1], dev(z, x, c, (y + o) % 4))
    for o in range(1, 8):
        remote(
            sel_out.at[(w + o) % 8], small.at[slab], send_sem.at[11], norm_sem.at[2], xc_peer(o)
        )
    small[slab] = sel_out[w]
    drain(sq2.at[pl.ds(0, 3)], norm_sem.at[1])
    squares_total = jnp.sum(jnp.sum(sq2[...], axis=0), keepdims=True)
    limit = jnp.float32(1024.0)
    scale = limit / jnp.maximum(jnp.sqrt(squares_total), limit)
    rounded = adam(summed, *states, scale, first_fix, second_fix)[0].astype(BF16)

    for f in FLOWS:
        along_x, p, qq, c1, c2, peer1, peer2 = flows[f]
        w_part[f, c1, c2] = rounded[64 * f : 64 * f + 64]
        own = w_part.at[f, c1, c2]
        for o in (2, 1, 3):
            remote(own, own, send_sem.at[12], ag2_sem.at[f], peer2((c2 + o) % 4))
    small[8] = jnp.broadcast_to(scale, (4, 128))

    def give(f, index):
        piece = w_part.at[f, index]
        remote(piece, w_all.at[c, f, index], send_sem.at[14], out_sem.at[0], partner)
        pltpu.make_async_copy(piece, w_all.at[c, f, index], out_sem.at[1]).start()

    wide = {}
    for f in FLOWS:
        along_x, p, qq, c1, c2, peer1, peer2 = flows[f]
        drain(w_part.at[f, c1, pl.ds(0, 3)], ag2_sem.at[f])
        own = w_part.at[f, c1]
        wide[f, 0] = remote(own, own, send_sem.at[13], ag1_sem.at[f, 0], peer1(qq))
        wide[f, 1] = remote(own, own, send_sem.at[13], ag1_sem.at[f, 1], peer1(p))
        give(f, c1)
    for f in FLOWS:
        along_x, p, qq, c1, c2, peer1, peer2 = flows[f]
        wide[f, 0].wait_recv()
        got = w_part.at[f, qq]
        wide[f, 2] = remote(got, got, send_sem.at[13], ag1_sem.at[f, 2], peer1(p))
        give(f, qq)
    for f in FLOWS:
        wide[f, 1].wait_recv()
        give(f, flows[f][1])
    for f in FLOWS:
        wide[f, 2].wait_recv()
        give(f, flip2(flows[f][3]))

    drain(small.at[pl.ds(0, 7)], norm_sem.at[2])
    drain(opt_in.at[pl.ds(1, 7)], send_sem.at[0])
    drain(in1x, send_sem.at[1])
    drain(in1y, send_sem.at[2])
    drain(opt_all.at[pl.ds(0, 15)], send_sem.at[3])
    drain(core_out, send_sem.at[4])
    drain(in2, send_sem.at[5])
    drain(in3, send_sem.at[6])
    drain(zin.at[pl.ds(1, 15)], send_sem.at[7])
    drain(sums.at[pl.ds(0, 15)], send_sem.at[8])
    drain(sq1.at[pl.ds(0, 7)], send_sem.at[9])
    drain(sq2.at[pl.ds(0, 3)], send_sem.at[10])
    drain(sel_out.at[pl.ds(0, 7)], send_sem.at[11])
    drain(w_part.at[0, pl.ds(0, 3)], send_sem.at[12])
    drain(w_part.at[pl.ds(0, 3)], send_sem.at[13])
    drain(w_part, send_sem.at[14])
    drain(w_part, out_sem.at[1])
    drain(w_all.at[1 - c], out_sem.at[0])


def result_kernel(
    w_ref, small, step_ref, master_ref, first_ref, second_ref, w_out, nm_out, nf_out, ns_out, tmp
):
    f = pl.program_id(0)

    def assemble(along_x):
        for core in range(2):
            for k in range(4):
                for r in range(4):
                    i, j = (k, r) if along_x else (r, k)
                    tmp[k, pl.ds(r, 64, stride=4), :] = w_ref[core, 0, i, j].astype(F32)
                at = 512 * core + 128 * k
                w_out[:, at : at + 128] = tmp[k].astype(BF16)

    @pl.when(f % 2 == 0)
    def _():
        assemble(True)

    @pl.when(f % 2 == 1)
    def _():
        assemble(False)

    @pl.when(f == 0)
    def _():
        scale = small[8, :1, :1]
        filled = small[9] > 0.5
        fixes = corrections(step_ref)
        for k in range(8):
            cols = slice(128 * k, 128 * k + 128)
            olds = (master_ref[0, :, cols], first_ref[0, :, cols], second_ref[0, :, cols])
            parts = adam(small[k], *olds, scale, *fixes)
            for out, value in zip((nm_out, nf_out, ns_out), parts):
                out[0, :, cols] = jnp.where(filled, value, 0.0)


def local_step(gradient, owner_list, step_count, master, first_moment, second_moment):
    vmem = pl.BlockSpec(memory_space=pltpu.VMEM)
    smem = pl.BlockSpec(memory_space=pltpu.SMEM)
    anywhere = pl.BlockSpec(memory_space=pl.ANY)
    dma = pltpu.SemaphoreType.DMA
    w_all, small = pl.pallas_call(
        reduce_kernel,
        out_shape=(
            jax.ShapeDtypeStruct((2, 4, 4, 4, 64, 128), BF16),
            jax.ShapeDtypeStruct((10, 4, 128), F32),
        ),
        in_specs=[anywhere, vmem, smem, vmem, vmem, vmem],
        out_specs=(anywhere, vmem),
        scratch_shapes=[
            pltpu.VMEM((1024, 1024), BF16),
            pltpu.VMEM((2, 4, 2, 4, 64, 128), BF16),
            pltpu.VMEM((2, 256, 128), F32),
            pltpu.VMEM((2, 4, 256, 128), BF16),
            pltpu.VMEM((2, 4, 4, 64, 128), BF16),
            pltpu.VMEM((4, 2, 4, 64, 128), F32),
            pltpu.VMEM((4, 2, 4, 64, 128), F32),
            pltpu.VMEM((4, 4, 4, 64, 128), F32),
            pltpu.VMEM((4, 4, 64, 128), F32),
            pltpu.VMEM((4, 3, 64, 128), F32),
            pltpu.VMEM((NZ, 16, 128), F32),
            pltpu.VMEM((NZ, 16, 128), F32),
            pltpu.VMEM((NZ, 16, 128), F32),
            pltpu.VMEM((8, 8, 128), F32),
            pltpu.VMEM((4, 8, 128), F32),
            pltpu.VMEM((8, 4, 128), F32),
            pltpu.VMEM((8, 3, 4, 128), F32),
            pltpu.VMEM((8, 3, 4, 128), F32),
            pltpu.VMEM((NZ, 3, 32, 128), F32),
            pltpu.VMEM((256, 512), F32),
            pltpu.VMEM((4, 4, 4, 64, 128), BF16),
            dma((4,)),
            dma((4, 4)),
            dma((4, 2)),
            dma((4,)),
            dma((4,)),
            dma((1,)),
            dma((2, 8)),
            dma((2,)),
            dma((3,)),
            dma((4,)),
            dma((4, 3)),
            dma((2,)),
            dma((15,)),
        ],
        compiler_params=pltpu.CompilerParams(collective_id=0, has_side_effects=True),
        name="adam_reduce",
    )(
        gradient.reshape(gradient.shape[2:]),
        owner_list.reshape(1, owner_list.shape[0]),
        step_count,
        master,
        first_moment,
        second_moment,
    )
    state = jax.ShapeDtypeStruct(master.shape, F32)
    state_block = pl.BlockSpec(master.shape, lambda f: (0, 0, 0))
    return pl.pallas_call(
        result_kernel,
        grid=(4,),
        out_shape=(jax.ShapeDtypeStruct((1024, 1024), BF16), state, state, state),
        in_specs=[
            pl.BlockSpec((2, 1, 4, 4, 64, 128), lambda f: (0, f, 0, 0, 0, 0)),
            pl.BlockSpec((10, 4, 128), lambda f: (0, 0, 0)),
            smem,
            state_block,
            state_block,
            state_block,
        ],
        out_specs=(pl.BlockSpec((256, 1024), lambda f: (f, 0)), state_block, state_block, state_block),
        scratch_shapes=[pltpu.VMEM((4, 256, 128), F32)],
        name="adam_results",
    )(w_all, small, step_count, master, first_moment, second_moment)


def solution(mesh):
    owned = P("dp", None, "rep")
    return jax.shard_map(
        local_step,
        mesh=mesh,
        in_specs=(P("dp", "rep", None, None), P(), P(), owned, owned, owned),
        out_specs=(P(), owned, owned, owned),
        check_vma=False,
    )
```

time: 553 us -> 92.9 us (0.17)
  blocking collectives: 318 us -> 0 us
  waiting for transfers between devices: 175 us -> 0 us
  Pallas kernels: 0 us -> 91.3 us
  local copies, waits for them, and re-layouts: 34.1 us -> 0 us
  between operations: 15.6 us -> 1.29 us
  other arithmetic: 9.06 us -> 0 us
    all_to_all x1 -> x0, blocking collectives: 204 us -> none  [local(): lax.all_to_all(outgoing, 'dp', split_axis=0, concat_axis=0, tiled=True)]
    all_gather x1 -> x0, waiting for transfers between devices: 141 us -> none  [local(): collected = lax.all_gather(joined[None], 'dp', axis=0, tiled=True)]
    psum x1 -> x0, blocking collectives: 104 us -> none  [local(): squares_total = lax.psum(jnp.sum(owned_sum * owned_sum), ('dp', 'rep'))]
    pallas_call x0 -> x2, Pallas kernels: none -> 91.3 us  [the longest x1 87 us: local_step(): pl.pallas_call(reduce_kernel, out_shape=(jax.ShapeDtypeStruct((2, 4, 4, 4...]
    unnamed x3 -> x0, waiting for transfers between devices: 34.8 us -> none
    gather x3 -> x0, local copies, waits for them, and re-layouts: 18.2 us -> none  [the longest x2 11.5 us: local(): blocks[picked]]
    unnamed x11 -> x0, local copies, waits for them, and re-layouts: 10.1 us -> none
    all_gather x1 -> x0, blocking collectives: 10.1 us -> none  [local(): joined = lax.all_gather(rounded, 'rep', axis=1, tiled=True)]
  transfers between devices with their start and end apart: 2 -> 0, of which waited for: 2 -> 0; matrix products, arithmetic and copies ran while one was open for 0% -> 0% of each run, Pallas kernels for 0% -> 0%
where the time goes in v2:
time: 92.9 us; the launch traced here: 92.6 us
  Pallas kernels  91.3 us (98%)
  between operations  1.29 us (1%)
    pallas_call x1, Pallas kernels, local_step(): pl.pallas_call(reduce_kernel, out_shape=(jax.ShapeDtypeStruct((2, 4, 4, 4...  87 us
    pallas_call x1, Pallas kernels, local_step(): pl.pallas_call(result_kernel, grid=(4,), out_shape=(jax.ShapeDtypeStruct(...  4.28 us

profile of v2, /device:TPU:1, one launch (start us, length us, event | category | flops | bytes accessed | tf_op | source)
XLA Modules:
  0.0 92.6 jit_solution(3571418612925292072)
XLA Ops:
  1.3 87.0 %adam_reduce.1 = (bf16[2,4,4,4,64,128]{5,4,3,2,1,0:T(8,128)(2,1)}, f32[10,4,128]{2,1,0:T(4,128)}) custom-call(bf16[1024,1024]{1,0:T(8,128)(2,1)} %bitcast.2, s32[1,256]{1,0:T(1,128)} %bitcast.3, s32[1]{0:T(128)S(6)} %copy.10.step_ref, f32[1,4,1024]{2,1,0:T(4,128)} %master_ref.3, f32[1,4,1024]{2,1,0:T(4,128)} %first_ref.3, f32[1,4,1024]{2,1,0:T(4,128)} %second_ref.3), custom_call_target="tpu_custom_call" | custom-call | tf_op jit(solution)/shard_map/adam_reduce/pallas_call | solution.py:454
  88.3 4.3 %adam_results.1 = (bf16[1024,1024]{1,0:T(8,128)(2,1)}, f32[1,4,1024]{2,1,0:T(4,128)}, f32[1,4,1024]{2,1,0:T(4,128)}, f32[1,4,1024]{2,1,0:T(4,128)}) custom-call(bf16[2,4,4,4,64,128]{5,4,3,2,1,0:T(8,128)(2,1)} %get-tuple-element.6.w_ref, f32[10,4,128]{2,1,0:T(4,128)} %get-tuple-element.7.small, s32[1]{0:T(128)S(6)} %copy.10.step_ref, ...), custom_call_target="tpu_custom_call" | custom-call | tf_op jit(solution)/shard_map/adam_results/pallas_call | solution.py:510

commit v3 on v2

--- a/solution.py
+++ b/solution.py
@@ -91,6 +91,7 @@
     ag1_sem,
     out_sem,
     send_sem,
+    token_sem,
 ):
     d = lax.axis_index("dp")
     y = lax.axis_index("rep")
@@ -202,6 +203,12 @@
             opt_all[z, a, pl.ds(ws * 4, 4), :] = opt_in[o, a]
     ring_r = []
     ring_l = []
+
+    def token(i, distance):
+        for to in ((z + distance) % NZ, (z + NZ - distance) % NZ):
+            pl.semaphore_signal(
+                token_sem.at[i], inc=1, device_id=dev(to, x, c, y), device_id_type=MESH
+            )
 
     def ring_step():
         s = len(ring_r) + 1
@@ -267,7 +274,6 @@
         to_core(f, 0)
     for f in FLOWS:
         keep(f, 0)
-    ring_step()
     for f in FLOWS:
         along_x, p, qq, c1, c2, peer1, peer2 = flows[f]
         core[f, 0].wait_recv()
@@ -278,6 +284,7 @@
     for f in FLOWS:
         to_core(f, 1)
     ring_step()
+    token(0, 2)
 
     row_id = lax.broadcasted_iota(jnp.int32, (256, 256), 0)
     col_id = lax.broadcasted_iota(jnp.int32, (256, 256), 1)
@@ -295,7 +302,6 @@
 
     for f in FLOWS:
         keep(f, 1)
-    ring_step()
     for f in FLOWS:
         along_x, p, qq, c1, c2, peer1, peer2 = flows[f]
         core[f, 1].wait_recv()
@@ -307,32 +313,31 @@
                 part.at[f, c1, to], in3.at[f, o - 1], send_sem.at[6], dim2_sem.at[f], peer2(to)
             )
     ring_step()
-    ring_step()
+    pl.semaphore_wait(token_sem.at[0], 2)
+    token(1, 4)
     for f in FLOWS:
         along_x, p, qq, c1, c2, peer1, peer2 = flows[f]
         drain(in3.at[f], dim2_sem.at[f])
         total = part[f, c1, c2] + in3[f, 0] + in3[f, 1] + in3[f, 2]
         for k in range(4):
             zsend[4 * f + k] = total[16 * k : 16 * k + 16]
-    ring_step()
-    ring_step()
-    ring_step()
+    pl.semaphore_wait(token_sem.at[1], 2)
 
     order = [8, 7, 9, 6, 10, 5, 11, 4, 12, 3, 13, 2, 14, 1, 15]
     for o in order:
         to = (z + o) % NZ
         remote(zsend.at[to], zin.at[o], send_sem.at[7], z_sem.at[0], dev(to, x, c, y))
     zin[0] = zsend[z]
-    states = []
-    for a in range(3):
-        table = opt_all[:, a].reshape(512, 128)
-        states.append(jnp.dot(onehot[...], table, precision=HIGH, preferred_element_type=F32))
     first_fix, second_fix = corrections(step_ref)
+    ring_step()
+    ring_step()
     drain(zin.at[pl.ds(1, 15)], z_sem.at[0])
     sums[z] = jnp.sum(zin[...], axis=0)
     for o in order:
         to = (z + o) % NZ
         remote(sums.at[z], sums.at[z], send_sem.at[8], z_sem.at[1], dev(to, x, c, y))
+    ring_step()
+    ring_step()
     drain(sums.at[pl.ds(0, 15)], z_sem.at[1])
 
     summed = sums[...].reshape(256, 128)
@@ -342,6 +347,7 @@
     picked = jnp.dot(chosen, summed, precision=HIGH, preferred_element_type=F32)
     for k in range(8):
         sel_out[k] = picked[4 * k : 4 * k + 4]
+    ring_step()
     drain(sq1.at[pl.ds(0, 7)], norm_sem.at[0])
     sq2[y] = jnp.sum(sq1[...], axis=0)
     for o in (2, 1, 3):
@@ -351,18 +357,34 @@
             sel_out.at[(w + o) % 8], small.at[slab], send_sem.at[11], norm_sem.at[2], xc_peer(o)
         )
     small[slab] = sel_out[w]
+    ring_step()
+    states = []
+    for a in range(3):
+        table = opt_all[:, a].reshape(512, 128)
+        states.append(jnp.dot(onehot[...], table, precision=HIGH, preferred_element_type=F32))
     drain(sq2.at[pl.ds(0, 3)], norm_sem.at[1])
     squares_total = jnp.sum(jnp.sum(sq2[...], axis=0), keepdims=True)
     limit = jnp.float32(1024.0)
     scale = limit / jnp.maximum(jnp.sqrt(squares_total), limit)
     rounded = adam(summed, *states, scale, first_fix, second_fix)[0].astype(BF16)
 
+    def forward(f, j):
+        along_x, p, qq, c1, c2, peer1, peer2 = flows[f]
+        piece = w_part.at[f, c1, j]
+        remote(piece, piece, send_sem.at[13], ag1_sem.at[f, 0], peer1(qq))
+        remote(piece, piece, send_sem.at[13], ag1_sem.at[f, 1], peer1(p))
+
+    ag2 = {}
     for f in FLOWS:
         along_x, p, qq, c1, c2, peer1, peer2 = flows[f]
         w_part[f, c1, c2] = rounded[64 * f : 64 * f + 64]
         own = w_part.at[f, c1, c2]
         for o in (2, 1, 3):
-            remote(own, own, send_sem.at[12], ag2_sem.at[f], peer2((c2 + o) % 4))
+            ag2[f, o] = remote(
+                own, own, send_sem.at[12], ag2_sem.at[f, o - 1], peer2((c2 + o) % 4)
+            )
+    for f in FLOWS:
+        forward(f, flows[f][4])
     small[8] = jnp.broadcast_to(scale, (4, 128))
 
     def give(f, index):
@@ -370,25 +392,25 @@
         remote(piece, w_all.at[c, f, index], send_sem.at[14], out_sem.at[0], partner)
         pltpu.make_async_copy(piece, w_all.at[c, f, index], out_sem.at[1]).start()
 
-    wide = {}
-    for f in FLOWS:
-        along_x, p, qq, c1, c2, peer1, peer2 = flows[f]
-        drain(w_part.at[f, c1, pl.ds(0, 3)], ag2_sem.at[f])
-        own = w_part.at[f, c1]
-        wide[f, 0] = remote(own, own, send_sem.at[13], ag1_sem.at[f, 0], peer1(qq))
-        wide[f, 1] = remote(own, own, send_sem.at[13], ag1_sem.at[f, 1], peer1(p))
-        give(f, c1)
-    for f in FLOWS:
-        along_x, p, qq, c1, c2, peer1, peer2 = flows[f]
-        wide[f, 0].wait_recv()
+    for o in (1, 3, 2):
+        for f in FLOWS:
+            ag2[f, o].wait_recv()
+            forward(f, (flows[f][4] + 4 - o) % 4)
+    for f in FLOWS:
+        give(f, flows[f][3])
+    for f in FLOWS:
+        along_x, p, qq, c1, c2, peer1, peer2 = flows[f]
         got = w_part.at[f, qq]
-        wide[f, 2] = remote(got, got, send_sem.at[13], ag1_sem.at[f, 2], peer1(p))
+        drain(got, ag1_sem.at[f, 0])
+        remote(got, got, send_sem.at[13], ag1_sem.at[f, 2], peer1(p))
         give(f, qq)
     for f in FLOWS:
-        wide[f, 1].wait_recv()
+        got = w_part.at[f, flows[f][1]]
+        drain(got, ag1_sem.at[f, 1])
         give(f, flows[f][1])
     for f in FLOWS:
-        wide[f, 2].wait_recv()
+        got = w_part.at[f, flip2(flows[f][3])]
+        drain(got, ag1_sem.at[f, 2])
         give(f, flip2(flows[f][3]))
 
     drain(small.at[pl.ds(0, 7)], norm_sem.at[2])
@@ -412,38 +434,54 @@
 
 
 def result_kernel(
-    w_ref, small, step_ref, master_ref, first_ref, second_ref, w_out, nm_out, nf_out, ns_out, tmp
+    w_all,
+    small,
+    step_ref,
+    master_ref,
+    first_ref,
+    second_ref,
+    w_out,
+    nm_out,
+    nf_out,
+    ns_out,
+    w_in,
+    rows,
+    tmp,
+    in_sem,
+    out_sem,
 ):
-    f = pl.program_id(0)
-
-    def assemble(along_x):
+    loads = {}
+    for f in range(4):
         for core in range(2):
+            loads[f, core] = pltpu.make_async_copy(
+                w_all.at[core, f], w_in.at[core, f], in_sem.at[f, core]
+            )
+            loads[f, core].start()
+    scale = small[8, :1, :1]
+    filled = small[9] > 0.5
+    fixes = corrections(step_ref)
+    for k in range(8):
+        cols = slice(128 * k, 128 * k + 128)
+        olds = (master_ref[0, :, cols], first_ref[0, :, cols], second_ref[0, :, cols])
+        parts = adam(small[k], *olds, scale, *fixes)
+        for out, value in zip((nm_out, nf_out, ns_out), parts):
+            out[0, :, cols] = jnp.where(filled, value, 0.0)
+    stores = []
+    for f in range(4):
+        for core in range(2):
+            loads[f, core].wait()
             for k in range(4):
                 for r in range(4):
-                    i, j = (k, r) if along_x else (r, k)
-                    tmp[k, pl.ds(r, 64, stride=4), :] = w_ref[core, 0, i, j].astype(F32)
+                    i, j = (k, r) if f % 2 == 0 else (r, k)
+                    tmp[k, pl.ds(r, 64, stride=4), :] = w_in[core, f, i, j].astype(F32)
                 at = 512 * core + 128 * k
-                w_out[:, at : at + 128] = tmp[k].astype(BF16)
-
-    @pl.when(f % 2 == 0)
-    def _():
-        assemble(True)
-
-    @pl.when(f % 2 == 1)
-    def _():
-        assemble(False)
-
-    @pl.when(f == 0)
-    def _():
-        scale = small[8, :1, :1]
-        filled = small[9] > 0.5
-        fixes = corrections(step_ref)
-        for k in range(8):
-            cols = slice(128 * k, 128 * k + 128)
-            olds = (master_ref[0, :, cols], first_ref[0, :, cols], second_ref[0, :, cols])
-            parts = adam(small[k], *olds, scale, *fixes)
-            for out, value in zip((nm_out, nf_out, ns_out), parts):
-                out[0, :, cols] = jnp.where(filled, value, 0.0)
+                rows[f, :, at : at + 128] = tmp[k].astype(BF16)
+        stores.append(
+            pltpu.make_async_copy(rows.at[f], w_out.at[pl.ds(256 * f, 256)], out_sem.at[f])
+        )
+        stores[f].start()
+    for store in stores:
+        store.wait()
 
 
 def local_step(gradient, owner_list, step_count, master, first_moment, second_moment):
@@ -490,10 +528,11 @@
             dma((2, 8)),
             dma((2,)),
             dma((3,)),
-            dma((4,)),
+            dma((4, 3)),
             dma((4, 3)),
             dma((2,)),
             dma((15,)),
+            pltpu.SemaphoreType.REGULAR((2,)),
         ],
         compiler_params=pltpu.CompilerParams(collective_id=0, has_side_effects=True),
         name="adam_reduce",
@@ -506,21 +545,18 @@
         second_moment,
     )
     state = jax.ShapeDtypeStruct(master.shape, F32)
-    state_block = pl.BlockSpec(master.shape, lambda f: (0, 0, 0))
     return pl.pallas_call(
         result_kernel,
-        grid=(4,),
         out_shape=(jax.ShapeDtypeStruct((1024, 1024), BF16), state, state, state),
-        in_specs=[
-            pl.BlockSpec((2, 1, 4, 4, 64, 128), lambda f: (0, f, 0, 0, 0, 0)),
-            pl.BlockSpec((10, 4, 128), lambda f: (0, 0, 0)),
-            smem,
-            state_block,
-            state_block,
-            state_block,
+        in_specs=[anywhere, vmem, smem, vmem, vmem, vmem],
+        out_specs=(anywhere, vmem, vmem, vmem),
+        scratch_shapes=[
+            pltpu.VMEM((2, 4, 4, 4, 64, 128), BF16),
+            pltpu.VMEM((4, 256, 1024), BF16),
+            pltpu.VMEM((4, 256, 128), F32),
+            dma((4, 2)),
+            dma((4,)),
         ],
-        out_specs=(pl.BlockSpec((256, 1024), lambda f: (f, 0)), state_block, state_block, state_block),
-        scratch_shapes=[pltpu.VMEM((4, 256, 128), F32)],
         name="adam_results",
     )(w_all, small, step_count, master, first_moment, second_moment)
 

time: 92.9 us -> 78.8 us (0.85)
  Pallas kernels: 91.3 us -> 77 us
    pallas_call x1, Pallas kernels: 87 us -> 72.9 us  [local_step(): pl.pallas_call(reduce_kernel, out_shape=(jax.ShapeDtypeStruct((2, 4, 4, 4...]
where the time goes in v3:
time: 78.8 us; the launch traced here: 78.3 us
  Pallas kernels  77 us (98%)
  between operations  1.29 us (2%)
    pallas_call x1, Pallas kernels, local_step(): pl.pallas_call(reduce_kernel, out_shape=(jax.ShapeDtypeStruct((2, 4, 4, 4...  72.9 us
    pallas_call x1, Pallas kernels, local_step(): pl.pallas_call(result_kernel, out_shape=(jax.ShapeDtypeStruct((1024, 1024...  4.15 us

profile of v3, /device:TPU:1, one launch (start us, length us, event | category | flops | bytes accessed | tf_op | source)
XLA Modules:
  0.0 78.3 jit_solution(11866983120694836606)
XLA Ops:
  1.3 72.9 %adam_reduce.1 = (bf16[2,4,4,4,64,128]{5,4,3,2,1,0:T(8,128)(2,1)}, f32[10,4,128]{2,1,0:T(4,128)}) custom-call(bf16[1024,1024]{1,0:T(8,128)(2,1)} %bitcast.2, s32[1,256]{1,0:T(1,128)} %bitcast.3, s32[1]{0:T(128)S(6)} %copy.10.step_ref, f32[1,4,1024]{2,1,0:T(4,128)} %master_ref.3, f32[1,4,1024]{2,1,0:T(4,128)} %first_ref.3, f32[1,4,1024]{2,1,0:T(4,128)} %second_ref.3), custom_call_target="tpu_custom_call" | custom-call | tf_op jit(solution)/shard_map/adam_reduce/pallas_call | solution.py:492
  74.2 4.1 %adam_results.1 = (bf16[1024,1024]{1,0:T(8,128)(2,1)}, f32[1,4,1024]{2,1,0:T(4,128)}, f32[1,4,1024]{2,1,0:T(4,128)}, f32[1,4,1024]{2,1,0:T(4,128)}) custom-call(bf16[2,4,4,4,64,128]{5,4,3,2,1,0:T(8,128)(2,1)} %get-tuple-element.6.w_all, f32[10,4,128]{2,1,0:T(4,128)} %get-tuple-element.7.small, s32[1]{0:T(128)S(6)} %copy.10.step_ref, ...), custom_call_target="tpu_custom_call" | custom-call | tf_op jit(solution)/shard_map/adam_results/pallas_call | solution.py:548

commit v4 on v3

--- a/solution.py
+++ b/solution.py
@@ -11,6 +11,7 @@
 HIGH = lax.Precision.HIGHEST
 NZ = 16
 FLOWS = (0, 2, 1, 3)
+GATHERED = [(d, None) for d in range(-7, 8) if d] + [(-8, 0), (8, 1)]
 
 
 def flip1(v):
@@ -50,12 +51,15 @@
 
 def reduce_kernel(
     grad,
+    owner_hbm,
+    step_ref,
+    master_hbm,
+    first_hbm,
+    second_hbm,
+    w_all,
+    small_hbm,
     owner_ref,
-    step_ref,
-    master_ref,
-    first_ref,
-    second_ref,
-    w_all,
+    state_in,
     small,
     g,
     gy,
@@ -70,8 +74,7 @@
     zsend,
     zin,
     sums,
-    sq1,
-    sq2,
+    squares,
     sel_out,
     opt_out,
     opt_in,
@@ -84,7 +87,7 @@
     step2_sem,
     dim2_sem,
     opt_sem,
-    ring_sem,
+    gather_sem,
     z_sem,
     norm_sem,
     ag2_sem,
@@ -100,6 +103,7 @@
     x = w // 2
     c = d % 2
     slab = c * 4 + x
+    q = y * 8 + w
 
     def dev(zz, xx, cc, yy):
         return (zz * 8 + xx * 2 + cc, yy)
@@ -121,6 +125,17 @@
 
     partner = dev(z, x, 1 - c, y)
 
+    inputs = []
+    for i, (src, dst) in enumerate(
+        (
+            (master_hbm, state_in.at[0]),
+            (first_hbm, state_in.at[1]),
+            (second_hbm, state_in.at[2]),
+            (owner_hbm, owner_ref),
+        )
+    ):
+        inputs.append(pltpu.make_async_copy(src, dst, load_sem.at[4 + i]))
+        inputs[i].start()
     loads = {}
     for f in (1, 3, 0, 2):
         loads[f] = pltpu.make_async_copy(
@@ -141,19 +156,32 @@
     for device in near:
         pl.semaphore_signal(barrier, inc=1, device_id=device, device_id_type=MESH)
 
-    states_in = (master_ref, first_ref, second_ref)
+    for copy in inputs:
+        copy.wait()
     for k in range(8):
         for a in range(3):
-            opt_out[k, a] = states_in[a][0, :, 128 * k : 128 * k + 128]
+            opt_out[k % 4, k // 4, a] = state_in[a, 0, :, 128 * k : 128 * k + 128]
+
+    def token(i, distance):
+        for to in ((z + distance) % NZ, (z + NZ - distance) % NZ):
+            pl.semaphore_signal(
+                token_sem.at[i], inc=1, device_id=dev(to, x, c, y), device_id_type=MESH
+            )
 
     pl.semaphore_wait(barrier, len(near))
-
-    for o in range(1, 8):
-        t = (w + o) % 8
-        remote(
-            opt_out.at[(t % 2) * 4 + t // 2], opt_in.at[o], send_sem.at[0], opt_sem.at[0], xc_peer(o)
-        )
-    opt_in[0] = opt_out[slab]
+    token(0, 1)
+
+    for o in range(1, 4):
+        xt = (x + o) % 4
+        remote(opt_out.at[xt], opt_in.at[w], send_sem.at[0], opt_sem.at[0], dev(z, xt, 1, y))
+
+    @pl.when(c == 0)
+    def _():
+        remote(opt_out.at[x], opt_in.at[w], send_sem.at[0], opt_sem.at[0], partner)
+
+    @pl.when(c == 1)
+    def _():
+        opt_in[w] = opt_out[x]
 
     flows = []
     for f in range(4):
@@ -196,38 +224,55 @@
                 gy[f // 2, r, k // 4, k % 4] = tmp[k % 2, pl.ds(r, 64, stride=4), :].astype(BF16)
         send_step1(f)
 
-    drain(opt_in.at[pl.ds(1, 7)], opt_sem.at[0])
-    for o in range(8):
-        ws = (w + 8 - o) % 8
-        for a in range(3):
-            opt_all[z, a, pl.ds(ws * 4, 4), :] = opt_in[o, a]
-    ring_r = []
-    ring_l = []
-
-    def token(i, distance):
-        for to in ((z + distance) % NZ, (z + NZ - distance) % NZ):
-            pl.semaphore_signal(
-                token_sem.at[i], inc=1, device_id=dev(to, x, c, y), device_id_type=MESH
-            )
-
-    def ring_step():
-        s = len(ring_r) + 1
-        if s > 9:
-            return
-        if s > 1:
-            ring_r[s - 2].wait_recv()
-            if s - 2 < 7:
-                ring_l[s - 2].wait_recv()
-        if s <= 8:
-            at = opt_all.at[(z + NZ - s + 1) % NZ]
-            ring_r.append(remote(at, at, send_sem.at[3], ring_sem.at[0, s - 1], right))
-        else:
-            ring_r.append(None)
-        if s <= 7:
-            at = opt_all.at[(z + s - 1) % NZ]
-            ring_l.append(remote(at, at, send_sem.at[3], ring_sem.at[1, s - 1], left))
-
-    ring_step()
+    pl.semaphore_wait(token_sem.at[0], 2)
+    token(1, 2)
+
+    def pass_state(d, t, half=None):
+        src = opt_all.at[(z + d + NZ) % NZ]
+        if half is not None:
+            src = src.at[:, :, pl.ds(16 * half, 16)]
+        sem = gather_sem.at[GATHERED.index((d - t, half))]
+        remote(src, src, send_sem.at[3], sem, dev((z + t + NZ) % NZ, x, c, y))
+
+    def hand_over(d):
+        src = opt_all.at[(z + d + NZ) % NZ, 0]
+        remote(src, src, send_sem.at[10], opt_sem.at[1], partner)
+
+    def take_state(*ds):
+        for d in ds:
+            if d == 8:
+                for half in range(2):
+                    drain(
+                        opt_all.at[0, :, :, pl.ds(0, 16)],
+                        gather_sem.at[GATHERED.index((8 * half * 2 - 8, half))],
+                    )
+            else:
+                drain(opt_all.at[0], gather_sem.at[GATHERED.index((d, None))])
+
+    def relay(s):
+        for d in (-s, s):
+            take_state(d)
+            if s < 7:
+                pass_state(d, 1 if d < 0 else -1)
+            else:
+                pass_state(d, 1 if d < 0 else -1, (d + 7) // 14)
+        hand_over(-s)
+        hand_over(s)
+
+    pl.semaphore_wait(token_sem.at[1], 2)
+    token(2, 4)
+
+    @pl.when(c == 1)
+    def _():
+        drain(opt_in.at[pl.ds(0, 7)], opt_sem.at[0])
+        for ws in range(8):
+            for side in range(2):
+                for a in range(3):
+                    opt_all[z, side, a, 4 * ws : 4 * ws + 4] = opt_in[ws, side, a]
+        for t in (1, -1, 4, -4):
+            pass_state(0, t)
+        hand_over(0)
+
     loads[0].wait()
     loads[2].wait()
 
@@ -281,10 +326,12 @@
         step2[f] = remote(
             part.at[f, qq], in2.at[f], send_sem.at[5], step2_sem.at[f], peer1(qq)
         )
+    @pl.when(c == 1)
+    def _():
+        relay(1)
+
     for f in FLOWS:
         to_core(f, 1)
-    ring_step()
-    token(0, 2)
 
     row_id = lax.broadcasted_iota(jnp.int32, (256, 256), 0)
     col_id = lax.broadcasted_iota(jnp.int32, (256, 256), 1)
@@ -312,58 +359,83 @@
             remote(
                 part.at[f, c1, to], in3.at[f, o - 1], send_sem.at[6], dim2_sem.at[f], peer2(to)
             )
-    ring_step()
-    pl.semaphore_wait(token_sem.at[0], 2)
-    token(1, 4)
+        if f == 0:
+
+            @pl.when(c == 1)
+            def _():
+                for d in (-4, 4):
+                    take_state(d)
+                    pass_state(d, 1 if d < 0 else -1)
+                    pass_state(d, -1 if d < 0 else 1)
+                    hand_over(d)
+
     for f in FLOWS:
         along_x, p, qq, c1, c2, peer1, peer2 = flows[f]
         drain(in3.at[f], dim2_sem.at[f])
         total = part[f, c1, c2] + in3[f, 0] + in3[f, 1] + in3[f, 2]
         for k in range(4):
             zsend[4 * f + k] = total[16 * k : 16 * k + 16]
-    pl.semaphore_wait(token_sem.at[1], 2)
+    pl.semaphore_wait(token_sem.at[2], 2)
 
     order = [8, 7, 9, 6, 10, 5, 11, 4, 12, 3, 13, 2, 14, 1, 15]
     for o in order:
         to = (z + o) % NZ
         remote(zsend.at[to], zin.at[o], send_sem.at[7], z_sem.at[0], dev(to, x, c, y))
     zin[0] = zsend[z]
+
+    @pl.when(c == 1)
+    def _():
+        relay(5)
+        relay(6)
+
     first_fix, second_fix = corrections(step_ref)
-    ring_step()
-    ring_step()
     drain(zin.at[pl.ds(1, 15)], z_sem.at[0])
     sums[z] = jnp.sum(zin[...], axis=0)
     for o in order:
         to = (z + o) % NZ
         remote(sums.at[z], sums.at[z], send_sem.at[8], z_sem.at[1], dev(to, x, c, y))
-    ring_step()
-    ring_step()
+
+    @pl.when(c == 1)
+    def _():
+        for d in (-2, 2, -3, 3):
+            take_state(d)
+            hand_over(d)
+        relay(7)
+        take_state(8)
+        hand_over(8)
+
     drain(sums.at[pl.ds(0, 15)], z_sem.at[1])
 
     summed = sums[...].reshape(256, 128)
-    sq1[w] = jnp.sum((summed * summed).reshape(32, 8, 128), axis=0)
-    for o in range(1, 8):
-        remote(sq1.at[w], sq1.at[w], send_sem.at[9], norm_sem.at[0], xc_peer(o))
+    squares[q] = jnp.sum(summed * summed, axis=0, keepdims=True)
+    for o in range(1, 32):
+        t = (q + o) % 32
+        remote(
+            squares.at[q],
+            squares.at[q],
+            send_sem.at[9],
+            norm_sem.at[0],
+            dev(z, (t // 2) % 4, t % 2, t // 8),
+        )
     picked = jnp.dot(chosen, summed, precision=HIGH, preferred_element_type=F32)
     for k in range(8):
         sel_out[k] = picked[4 * k : 4 * k + 4]
-    ring_step()
-    drain(sq1.at[pl.ds(0, 7)], norm_sem.at[0])
-    sq2[y] = jnp.sum(sq1[...], axis=0)
-    for o in (2, 1, 3):
-        remote(sq2.at[y], sq2.at[y], send_sem.at[10], norm_sem.at[1], dev(z, x, c, (y + o) % 4))
     for o in range(1, 8):
         remote(
-            sel_out.at[(w + o) % 8], small.at[slab], send_sem.at[11], norm_sem.at[2], xc_peer(o)
+            sel_out.at[(w + o) % 8], small.at[slab], send_sem.at[11], norm_sem.at[1], xc_peer(o)
         )
     small[slab] = sel_out[w]
-    ring_step()
+
+    @pl.when(c == 0)
+    def _():
+        drain(opt_all.at[pl.ds(0, 8)], opt_sem.at[1])
+
     states = []
     for a in range(3):
-        table = opt_all[:, a].reshape(512, 128)
+        table = opt_all[:, c, a].reshape(512, 128)
         states.append(jnp.dot(onehot[...], table, precision=HIGH, preferred_element_type=F32))
-    drain(sq2.at[pl.ds(0, 3)], norm_sem.at[1])
-    squares_total = jnp.sum(jnp.sum(sq2[...], axis=0), keepdims=True)
+    drain(squares.at[pl.ds(0, 31)], norm_sem.at[0])
+    squares_total = jnp.sum(jnp.sum(squares[...], axis=0), keepdims=True)
     limit = jnp.float32(1024.0)
     scale = limit / jnp.maximum(jnp.sqrt(squares_total), limit)
     rounded = adam(summed, *states, scale, first_fix, second_fix)[0].astype(BF16)
@@ -398,6 +470,9 @@
             forward(f, (flows[f][4] + 4 - o) % 4)
     for f in FLOWS:
         give(f, flows[f][3])
+    drain(small.at[pl.ds(0, 7)], norm_sem.at[1])
+    small_copy = pltpu.make_async_copy(small, small_hbm, out_sem.at[2])
+    small_copy.start()
     for f in FLOWS:
         along_x, p, qq, c1, c2, peer1, peer2 = flows[f]
         got = w_part.at[f, qq]
@@ -413,18 +488,26 @@
         drain(got, ag1_sem.at[f, 2])
         give(f, flip2(flows[f][3]))
 
-    drain(small.at[pl.ds(0, 7)], norm_sem.at[2])
-    drain(opt_in.at[pl.ds(1, 7)], send_sem.at[0])
+    small_copy.wait()
+
+    @pl.when(c == 0)
+    def _():
+        drain(opt_out, send_sem.at[0])
+
+    @pl.when(c == 1)
+    def _():
+        drain(opt_out.at[pl.ds(0, 3)], send_sem.at[0])
+        drain(opt_all.at[pl.ds(0, 15)], send_sem.at[3])
+        drain(opt_all.at[pl.ds(0, 8)], send_sem.at[10])
+
     drain(in1x, send_sem.at[1])
     drain(in1y, send_sem.at[2])
-    drain(opt_all.at[pl.ds(0, 15)], send_sem.at[3])
     drain(core_out, send_sem.at[4])
     drain(in2, send_sem.at[5])
     drain(in3, send_sem.at[6])
     drain(zin.at[pl.ds(1, 15)], send_sem.at[7])
     drain(sums.at[pl.ds(0, 15)], send_sem.at[8])
-    drain(sq1.at[pl.ds(0, 7)], send_sem.at[9])
-    drain(sq2.at[pl.ds(0, 3)], send_sem.at[10])
+    drain(squares.at[pl.ds(0, 31)], send_sem.at[9])
     drain(sel_out.at[pl.ds(0, 7)], send_sem.at[11])
     drain(w_part.at[0, pl.ds(0, 3)], send_sem.at[12])
     drain(w_part.at[pl.ds(0, 3)], send_sem.at[13])
@@ -435,21 +518,36 @@
 
 def result_kernel(
     w_all,
-    small,
+    small_hbm,
     step_ref,
-    master_ref,
-    first_ref,
-    second_ref,
+    master_hbm,
+    first_hbm,
+    second_hbm,
     w_out,
     nm_out,
     nf_out,
     ns_out,
+    small,
+    state_in,
+    state_out,
     w_in,
     rows,
     tmp,
+    load_sem,
     in_sem,
     out_sem,
 ):
+    inputs = []
+    for i, (src, dst) in enumerate(
+        (
+            (small_hbm, small),
+            (master_hbm, state_in.at[0]),
+            (first_hbm, state_in.at[1]),
+            (second_hbm, state_in.at[2]),
+        )
+    ):
+        inputs.append(pltpu.make_async_copy(src, dst, load_sem.at[i]))
+        inputs[i].start()
     loads = {}
     for f in range(4):
         for core in range(2):
@@ -457,16 +555,19 @@
                 w_all.at[core, f], w_in.at[core, f], in_sem.at[f, core]
             )
             loads[f, core].start()
+    fixes = corrections(step_ref)
+    for copy in inputs:
+        copy.wait()
     scale = small[8, :1, :1]
     filled = small[9] > 0.5
-    fixes = corrections(step_ref)
     for k in range(8):
         cols = slice(128 * k, 128 * k + 128)
-        olds = (master_ref[0, :, cols], first_ref[0, :, cols], second_ref[0, :, cols])
-        parts = adam(small[k], *olds, scale, *fixes)
-        for out, value in zip((nm_out, nf_out, ns_out), parts):
-            out[0, :, cols] = jnp.where(filled, value, 0.0)
+        olds = [state_in[a, 0, :, cols] for a in range(3)]
+        for a, value in enumerate(adam(small[k], *olds, scale, *fixes)):
+            state_out[a, 0, :, cols] = jnp.where(filled, value, 0.0)
     stores = []
+    for a, out in enumerate((nm_out, nf_out, ns_out)):
+        stores.append(pltpu.make_async_copy(state_out.at[a], out, out_sem.at[8 + a]))
     for f in range(4):
         for core in range(2):
             loads[f, core].wait()
@@ -476,16 +577,23 @@
                     tmp[k, pl.ds(r, 64, stride=4), :] = w_in[core, f, i, j].astype(F32)
                 at = 512 * core + 128 * k
                 rows[f, :, at : at + 128] = tmp[k].astype(BF16)
-        stores.append(
-            pltpu.make_async_copy(rows.at[f], w_out.at[pl.ds(256 * f, 256)], out_sem.at[f])
-        )
-        stores[f].start()
+            cols = pl.ds(512 * core, 512)
+            stores.append(
+                pltpu.make_async_copy(
+                    rows.at[f, :, cols],
+                    w_out.at[pl.ds(256 * f, 256), cols],
+                    out_sem.at[2 * f + core],
+                )
+            )
+            stores[-1].start()
+            if f == 0 and core == 0:
+                for store in stores[:3]:
+                    store.start()
     for store in stores:
         store.wait()
 
 
 def local_step(gradient, owner_list, step_count, master, first_moment, second_moment):
-    vmem = pl.BlockSpec(memory_space=pltpu.VMEM)
     smem = pl.BlockSpec(memory_space=pltpu.SMEM)
     anywhere = pl.BlockSpec(memory_space=pl.ANY)
     dma = pltpu.SemaphoreType.DMA
@@ -495,9 +603,12 @@
             jax.ShapeDtypeStruct((2, 4, 4, 4, 64, 128), BF16),
             jax.ShapeDtypeStruct((10, 4, 128), F32),
         ),
-        in_specs=[anywhere, vmem, smem, vmem, vmem, vmem],
-        out_specs=(anywhere, vmem),
+        in_specs=[anywhere, anywhere, smem, anywhere, anywhere, anywhere],
+        out_specs=(anywhere, anywhere),
         scratch_shapes=[
+            pltpu.VMEM((1, owner_list.shape[0]), jnp.int32),
+            pltpu.VMEM((3, *master.shape), F32),
+            pltpu.VMEM((10, 4, 128), F32),
             pltpu.VMEM((1024, 1024), BF16),
             pltpu.VMEM((2, 4, 2, 4, 64, 128), BF16),
             pltpu.VMEM((2, 256, 128), F32),
@@ -511,28 +622,27 @@
             pltpu.VMEM((NZ, 16, 128), F32),
             pltpu.VMEM((NZ, 16, 128), F32),
             pltpu.VMEM((NZ, 16, 128), F32),
-            pltpu.VMEM((8, 8, 128), F32),
-            pltpu.VMEM((4, 8, 128), F32),
+            pltpu.VMEM((32, 1, 128), F32),
             pltpu.VMEM((8, 4, 128), F32),
-            pltpu.VMEM((8, 3, 4, 128), F32),
-            pltpu.VMEM((8, 3, 4, 128), F32),
-            pltpu.VMEM((NZ, 3, 32, 128), F32),
+            pltpu.VMEM((4, 2, 3, 4, 128), F32),
+            pltpu.VMEM((8, 2, 3, 4, 128), F32),
+            pltpu.VMEM((NZ, 2, 3, 32, 128), F32),
             pltpu.VMEM((256, 512), F32),
             pltpu.VMEM((4, 4, 4, 64, 128), BF16),
-            dma((4,)),
+            dma((8,)),
             dma((4, 4)),
             dma((4, 2)),
             dma((4,)),
             dma((4,)),
-            dma((1,)),
-            dma((2, 8)),
             dma((2,)),
-            dma((3,)),
+            dma((16,)),
+            dma((2,)),
+            dma((2,)),
             dma((4, 3)),
             dma((4, 3)),
-            dma((2,)),
+            dma((3,)),
             dma((15,)),
-            pltpu.SemaphoreType.REGULAR((2,)),
+            pltpu.SemaphoreType.REGULAR((3,)),
         ],
         compiler_params=pltpu.CompilerParams(collective_id=0, has_side_effects=True),
         name="adam_reduce",
@@ -548,14 +658,18 @@
     return pl.pallas_call(
         result_kernel,
         out_shape=(jax.ShapeDtypeStruct((1024, 1024), BF16), state, state, state),
-        in_specs=[anywhere, vmem, smem, vmem, vmem, vmem],
-        out_specs=(anywhere, vmem, vmem, vmem),
+        in_specs=[anywhere, anywhere, smem, anywhere, anywhere, anywhere],
+        out_specs=(anywhere, anywhere, anywhere, anywhere),
         scratch_shapes=[
+            pltpu.VMEM((10, 4, 128), F32),
+            pltpu.VMEM((3, *master.shape), F32),
+            pltpu.VMEM((3, *master.shape), F32),
             pltpu.VMEM((2, 4, 4, 4, 64, 128), BF16),
             pltpu.VMEM((4, 256, 1024), BF16),
             pltpu.VMEM((4, 256, 128), F32),
+            dma((4,)),
             dma((4, 2)),
-            dma((4,)),
+            dma((11,)),
         ],
         name="adam_results",
     )(w_all, small, step_count, master, first_moment, second_moment)

time: 78.8 us -> 73.9 us (0.938)
  Pallas kernels: 77 us -> 72.5 us
    pallas_call x1, Pallas kernels: 72.9 us -> 69.2 us  [local_step(): pl.pallas_call(reduce_kernel, out_shape=(jax.ShapeDtypeStruct((2, 4, 4, 4...]
    pallas_call x1, Pallas kernels: 4.15 us -> 3.23 us  [local_step(): pl.pallas_call(result_kernel, out_shape=(jax.ShapeDtypeStruct((1024, 1024...]
where the time goes in v4:
time: 73.9 us; the launch traced here: 73.7 us
  Pallas kernels  72.5 us (98%)
  between operations  1.29 us (2%)
    pallas_call x1, Pallas kernels, local_step(): pl.pallas_call(reduce_kernel, out_shape=(jax.ShapeDtypeStruct((2, 4, 4, 4...  69.2 us
    pallas_call x1, Pallas kernels, local_step(): pl.pallas_call(result_kernel, out_shape=(jax.ShapeDtypeStruct((1024, 1024...  3.23 us

profile of v4, /device:TPU:1, one launch (start us, length us, event | category | flops | bytes accessed | tf_op | source)
XLA Modules:
  0.0 73.7 jit_solution(8622938867974103074)
XLA Ops:
  1.3 69.2 %adam_reduce.1 = (bf16[2,4,4,4,64,128]{5,4,3,2,1,0:T(8,128)(2,1)}, f32[10,4,128]{2,1,0:T(4,128)}) custom-call(bf16[1024,1024]{1,0:T(8,128)(2,1)} %bitcast.2, s32[1,256]{1,0:T(1,128)} %bitcast.3, s32[1]{0:T(128)S(6)} %copy.10.step_ref, f32[1,4,1024]{2,1,0:T(4,128)} %master_hbm.3, f32[1,4,1024]{2,1,0:T(4,128)} %first_hbm.3, f32[1,4,1024]{2,1,0:T(4,128)} %second_hbm.3), custom_call_target="tpu_custom_call" | custom-call | tf_op jit(solution)/shard_map/adam_reduce/pallas_call | solution.py:600
  70.5 3.2 %adam_results.1 = (bf16[1024,1024]{1,0:T(8,128)(2,1)}, f32[1,4,1024]{2,1,0:T(4,128)}, f32[1,4,1024]{2,1,0:T(4,128)}, f32[1,4,1024]{2,1,0:T(4,128)}) custom-call(bf16[2,4,4,4,64,128]{5,4,3,2,1,0:T(8,128)(2,1)} %get-tuple-element.6.w_all, f32[10,4,128]{2,1,0:T(4,128)} %get-tuple-element.7.small_hbm, s32[1]{0:T(128)S(6)} %copy.10.step_ref, ...), custom_call_target="tpu_custom_call" | custom-call | tf_op jit(solution)/shard_map/adam_results/pallas_call | solution.py:658

commit v5 on v4

--- a/solution.py
+++ b/solution.py
@@ -227,37 +227,35 @@
     pl.semaphore_wait(token_sem.at[0], 2)
     token(1, 2)
 
-    def pass_state(d, t, half=None):
-        src = opt_all.at[(z + d + NZ) % NZ]
+    def pass_state(d, t, side, half=None):
+        src = opt_all.at[(z + d + NZ) % NZ, side]
         if half is not None:
-            src = src.at[:, :, pl.ds(16 * half, 16)]
-        sem = gather_sem.at[GATHERED.index((d - t, half))]
+            src = src.at[:, pl.ds(16 * half, 16)]
+        sem = gather_sem.at[side, GATHERED.index((d - t, half))]
         remote(src, src, send_sem.at[3], sem, dev((z + t + NZ) % NZ, x, c, y))
 
     def hand_over(d):
         src = opt_all.at[(z + d + NZ) % NZ, 0]
         remote(src, src, send_sem.at[10], opt_sem.at[1], partner)
 
-    def take_state(*ds):
-        for d in ds:
-            if d == 8:
-                for half in range(2):
-                    drain(
-                        opt_all.at[0, :, :, pl.ds(0, 16)],
-                        gather_sem.at[GATHERED.index((8 * half * 2 - 8, half))],
-                    )
-            else:
-                drain(opt_all.at[0], gather_sem.at[GATHERED.index((d, None))])
+    def take_state(d, side):
+        if d == 8:
+            for half in range(2):
+                drain(
+                    opt_all.at[0, 0, :, pl.ds(0, 16)],
+                    gather_sem.at[side, GATHERED.index((16 * half - 8, half))],
+                )
+        else:
+            drain(opt_all.at[0, 0], gather_sem.at[side, GATHERED.index((d, None))])
 
     def relay(s):
-        for d in (-s, s):
-            take_state(d)
-            if s < 7:
-                pass_state(d, 1 if d < 0 else -1)
-            else:
-                pass_state(d, 1 if d < 0 else -1, (d + 7) // 14)
-        hand_over(-s)
-        hand_over(s)
+        for side in range(2):
+            for d in (-s, s):
+                take_state(d, side)
+                on = 1 if d < 0 else -1
+                pass_state(d, on, side, None if s < 7 else (d + 7) // 14)
+                if side == 0:
+                    hand_over(d)
 
     pl.semaphore_wait(token_sem.at[1], 2)
     token(2, 4)
@@ -269,8 +267,9 @@
             for side in range(2):
                 for a in range(3):
                     opt_all[z, side, a, 4 * ws : 4 * ws + 4] = opt_in[ws, side, a]
-        for t in (1, -1, 4, -4):
-            pass_state(0, t)
+        for side in range(2):
+            for t in (1, -1):
+                pass_state(0, t, side)
         hand_over(0)
 
     loads[0].wait()
@@ -363,11 +362,7 @@
 
             @pl.when(c == 1)
             def _():
-                for d in (-4, 4):
-                    take_state(d)
-                    pass_state(d, 1 if d < 0 else -1)
-                    pass_state(d, -1 if d < 0 else 1)
-                    hand_over(d)
+                relay(2)
 
     for f in FLOWS:
         along_x, p, qq, c1, c2, peer1, peer2 = flows[f]
@@ -375,6 +370,12 @@
         total = part[f, c1, c2] + in3[f, 0] + in3[f, 1] + in3[f, 2]
         for k in range(4):
             zsend[4 * f + k] = total[16 * k : 16 * k + 16]
+        if f == 0:
+
+            @pl.when(c == 1)
+            def _():
+                relay(3)
+
     pl.semaphore_wait(token_sem.at[2], 2)
 
     order = [8, 7, 9, 6, 10, 5, 11, 4, 12, 3, 13, 2, 14, 1, 15]
@@ -385,8 +386,8 @@
 
     @pl.when(c == 1)
     def _():
+        relay(4)
         relay(5)
-        relay(6)
 
     first_fix, second_fix = corrections(step_ref)
     drain(zin.at[pl.ds(1, 15)], z_sem.at[0])
@@ -397,12 +398,8 @@
 
     @pl.when(c == 1)
     def _():
-        for d in (-2, 2, -3, 3):
-            take_state(d)
-            hand_over(d)
+        relay(6)
         relay(7)
-        take_state(8)
-        hand_over(8)
 
     drain(sums.at[pl.ds(0, 15)], z_sem.at[1])
 
@@ -425,6 +422,13 @@
             sel_out.at[(w + o) % 8], small.at[slab], send_sem.at[11], norm_sem.at[1], xc_peer(o)
         )
     small[slab] = sel_out[w]
+
+    @pl.when(c == 1)
+    def _():
+        take_state(8, 0)
+        hand_over(8)
+        take_state(8, 1)
+
 
     @pl.when(c == 0)
     def _():
@@ -537,6 +541,13 @@
     in_sem,
     out_sem,
 ):
+    loads = {}
+    for f in range(4):
+        for core in range(2):
+            loads[f, core] = pltpu.make_async_copy(
+                w_all.at[core, f], w_in.at[core, f], in_sem.at[f, core]
+            )
+            loads[f, core].start()
     inputs = []
     for i, (src, dst) in enumerate(
         (
@@ -548,27 +559,26 @@
     ):
         inputs.append(pltpu.make_async_copy(src, dst, load_sem.at[i]))
         inputs[i].start()
-    loads = {}
+    fixes = corrections(step_ref)
+    stores = []
+
+    def store(src, dst):
+        stores.append(pltpu.make_async_copy(src, dst, out_sem.at[len(stores)]))
+        stores[-1].start()
+
     for f in range(4):
-        for core in range(2):
-            loads[f, core] = pltpu.make_async_copy(
-                w_all.at[core, f], w_in.at[core, f], in_sem.at[f, core]
-            )
-            loads[f, core].start()
-    fixes = corrections(step_ref)
-    for copy in inputs:
-        copy.wait()
-    scale = small[8, :1, :1]
-    filled = small[9] > 0.5
-    for k in range(8):
-        cols = slice(128 * k, 128 * k + 128)
-        olds = [state_in[a, 0, :, cols] for a in range(3)]
-        for a, value in enumerate(adam(small[k], *olds, scale, *fixes)):
-            state_out[a, 0, :, cols] = jnp.where(filled, value, 0.0)
-    stores = []
-    for a, out in enumerate((nm_out, nf_out, ns_out)):
-        stores.append(pltpu.make_async_copy(state_out.at[a], out, out_sem.at[8 + a]))
-    for f in range(4):
+        if f == 2:
+            for copy in inputs:
+                copy.wait()
+            scale = small[8, :1, :1]
+            filled = small[9] > 0.5
+            for k in range(8):
+                cols = slice(128 * k, 128 * k + 128)
+                olds = [state_in[a, 0, :, cols] for a in range(3)]
+                for a, value in enumerate(adam(small[k], *olds, scale, *fixes)):
+                    state_out[a, 0, :, cols] = jnp.where(filled, value, 0.0)
+            for a, out in enumerate((nm_out, nf_out, ns_out)):
+                store(state_out.at[a], out)
         for core in range(2):
             loads[f, core].wait()
             for k in range(4):
@@ -577,20 +587,10 @@
                     tmp[k, pl.ds(r, 64, stride=4), :] = w_in[core, f, i, j].astype(F32)
                 at = 512 * core + 128 * k
                 rows[f, :, at : at + 128] = tmp[k].astype(BF16)
-            cols = pl.ds(512 * core, 512)
-            stores.append(
-                pltpu.make_async_copy(
-                    rows.at[f, :, cols],
-                    w_out.at[pl.ds(256 * f, 256), cols],
-                    out_sem.at[2 * f + core],
-                )
-            )
-            stores[-1].start()
-            if f == 0 and core == 0:
-                for store in stores[:3]:
-                    store.start()
-    for store in stores:
-        store.wait()
+            half = pl.ds(512 * core, 512)
+            store(rows.at[f, :, half], w_out.at[pl.ds(256 * f, 256), half])
+    for copy in stores:
+        copy.wait()
 
 
 def local_step(gradient, owner_list, step_count, master, first_moment, second_moment):
@@ -635,7 +635,7 @@
             dma((4,)),
             dma((4,)),
             dma((2,)),
-            dma((16,)),
+            dma((2, 16)),
             dma((2,)),
             dma((2,)),
             dma((4, 3)),

time: 73.9 us -> 72.9 us (0.986)
  Pallas kernels: 72.5 us -> 71.4 us
where the time goes in v5:
time: 72.9 us; the launch traced here: 72.7 us
  Pallas kernels  71.4 us (98%)
  between operations  1.29 us (2%)
    pallas_call x1, Pallas kernels, local_step(): pl.pallas_call(reduce_kernel, out_shape=(jax.ShapeDtypeStruct((2, 4, 4, 4...  68.5 us
    pallas_call x1, Pallas kernels, local_step(): pl.pallas_call(result_kernel, out_shape=(jax.ShapeDtypeStruct((1024, 1024...  2.85 us

profile of v5, /device:TPU:1, one launch (start us, length us, event | category | flops | bytes accessed | tf_op | source)
XLA Modules:
  0.0 72.7 jit_solution(16598192525064298815)
XLA Ops:
  1.3 68.5 %adam_reduce.1 = (bf16[2,4,4,4,64,128]{5,4,3,2,1,0:T(8,128)(2,1)}, f32[10,4,128]{2,1,0:T(4,128)}) custom-call(bf16[1024,1024]{1,0:T(8,128)(2,1)} %bitcast.2, s32[1,256]{1,0:T(1,128)} %bitcast.3, s32[1]{0:T(128)S(6)} %copy.10.step_ref, f32[1,4,1024]{2,1,0:T(4,128)} %master_hbm.3, f32[1,4,1024]{2,1,0:T(4,128)} %first_hbm.3, f32[1,4,1024]{2,1,0:T(4,128)} %second_hbm.3), custom_call_target="tpu_custom_call" | custom-call | tf_op jit(solution)/shard_map/adam_reduce/pallas_call | solution.py:600
  69.8 2.8 %adam_results.1 = (bf16[1024,1024]{1,0:T(8,128)(2,1)}, f32[1,4,1024]{2,1,0:T(4,128)}, f32[1,4,1024]{2,1,0:T(4,128)}, f32[1,4,1024]{2,1,0:T(4,128)}) custom-call(bf16[2,4,4,4,64,128]{5,4,3,2,1,0:T(8,128)(2,1)} %get-tuple-element.6.w_all, f32[10,4,128]{2,1,0:T(4,128)} %get-tuple-element.7.small_hbm, s32[1]{0:T(128)S(6)} %copy.10.step_ref, ...), custom_call_target="tpu_custom_call" | custom-call | tf_op jit(solution)/shard_map/adam_results/pallas_call | solution.py:658

commit v6 on v5

--- a/solution.py
+++ b/solution.py
@@ -447,6 +447,7 @@
     def forward(f, j):
         along_x, p, qq, c1, c2, peer1, peer2 = flows[f]
         piece = w_part.at[f, c1, j]
+        remote(piece, piece, send_sem.at[13], ag1_sem.at[f, 2], peer1(flip2(c1)))
         remote(piece, piece, send_sem.at[13], ag1_sem.at[f, 0], peer1(qq))
         remote(piece, piece, send_sem.at[13], ag1_sem.at[f, 1], peer1(p))
 
@@ -481,7 +482,6 @@
         along_x, p, qq, c1, c2, peer1, peer2 = flows[f]
         got = w_part.at[f, qq]
         drain(got, ag1_sem.at[f, 0])
-        remote(got, got, send_sem.at[13], ag1_sem.at[f, 2], peer1(p))
         give(f, qq)
     for f in FLOWS:
         got = w_part.at[f, flows[f][1]]

time: 72.9 us -> 71.1 us (0.975)
  Pallas kernels: 71.4 us -> 69.6 us
    pallas_call x1, Pallas kernels: 68.5 us -> 66.8 us  [local_step(): pl.pallas_call(reduce_kernel, out_shape=(jax.ShapeDtypeStruct((2, 4, 4, 4...]
where the time goes in v6:
time: 71.1 us; the launch traced here: 70.9 us
  Pallas kernels  69.6 us (98%)
  between operations  1.29 us (2%)
    pallas_call x1, Pallas kernels, local_step(): pl.pallas_call(reduce_kernel, out_shape=(jax.ShapeDtypeStruct((2, 4, 4, 4...  66.8 us
    pallas_call x1, Pallas kernels, local_step(): pl.pallas_call(result_kernel, out_shape=(jax.ShapeDtypeStruct((1024, 1024...  2.85 us

profile of v6, /device:TPU:1, one launch (start us, length us, event | category | flops | bytes accessed | tf_op | source)
XLA Modules:
  0.0 70.9 jit_solution(5867414524185829191)
XLA Ops:
  1.3 66.8 %adam_reduce.1 = (bf16[2,4,4,4,64,128]{5,4,3,2,1,0:T(8,128)(2,1)}, f32[10,4,128]{2,1,0:T(4,128)}) custom-call(bf16[1024,1024]{1,0:T(8,128)(2,1)} %bitcast.2, s32[1,256]{1,0:T(1,128)} %bitcast.3, s32[1]{0:T(128)S(6)} %copy.10.step_ref, f32[1,4,1024]{2,1,0:T(4,128)} %master_hbm.3, f32[1,4,1024]{2,1,0:T(4,128)} %first_hbm.3, f32[1,4,1024]{2,1,0:T(4,128)} %second_hbm.3), custom_call_target="tpu_custom_call" | custom-call | tf_op jit(solution)/shard_map/adam_reduce/pallas_call | solution.py:600
  68.0 2.8 %adam_results.1 = (bf16[1024,1024]{1,0:T(8,128)(2,1)}, f32[1,4,1024]{2,1,0:T(4,128)}, f32[1,4,1024]{2,1,0:T(4,128)}, f32[1,4,1024]{2,1,0:T(4,128)}) custom-call(bf16[2,4,4,4,64,128]{5,4,3,2,1,0:T(8,128)(2,1)} %get-tuple-element.6.w_all, f32[10,4,128]{2,1,0:T(4,128)} %get-tuple-element.7.small_hbm, s32[1]{0:T(128)S(6)} %copy.10.step_ref, ...), custom_call_target="tpu_custom_call" | custom-call | tf_op jit(solution)/shard_map/adam_results/pallas_call | solution.py:658

commit v7 on v6

--- a/solution.py
+++ b/solution.py
@@ -341,7 +341,7 @@
     rank_row = jnp.sum(jnp.where(same & (row_id < col_id), 1.0, 0.0), axis=0, keepdims=True)
     pos_col = (owner_col * 4.0 + rank_col).astype(jnp.int32)
     pos_row = (owner_ref[...].astype(F32) * 4.0 + rank_row).astype(jnp.int32)
-    onehot[...] = (pos_col == lax.broadcasted_iota(jnp.int32, (256, 512), 1)).astype(F32)
+    onehot[...] = (pos_col == lax.broadcasted_iota(jnp.int32, (256, 512), 1)).astype(F32).astype(BF16)
     chosen = (pos_row == z * 32 + lax.broadcasted_iota(jnp.int32, (32, 256), 0)).astype(F32)
     mine = (pos_row == d * 4 + lax.broadcasted_iota(jnp.int32, (4, 256), 0)).astype(F32)
     small[9] = jnp.broadcast_to(jnp.sum(mine, axis=1, keepdims=True), (4, 128))
@@ -364,24 +364,34 @@
             def _():
                 relay(2)
 
+    pl.semaphore_wait(token_sem.at[2], 2)
+
+    def reduce_z(to):
+        @pl.when(z != to)
+        def _():
+            remote(
+                zsend.at[to],
+                zin.at[(to - z + NZ) % NZ],
+                send_sem.at[7],
+                z_sem.at[0],
+                dev(to, x, c, y),
+            )
+
     for f in FLOWS:
         along_x, p, qq, c1, c2, peer1, peer2 = flows[f]
         drain(in3.at[f], dim2_sem.at[f])
         total = part[f, c1, c2] + in3[f, 0] + in3[f, 1] + in3[f, 2]
         for k in range(4):
             zsend[4 * f + k] = total[16 * k : 16 * k + 16]
+        for k in range(4):
+            reduce_z(4 * f + k)
         if f == 0:
 
             @pl.when(c == 1)
             def _():
                 relay(3)
 
-    pl.semaphore_wait(token_sem.at[2], 2)
-
     order = [8, 7, 9, 6, 10, 5, 11, 4, 12, 3, 13, 2, 14, 1, 15]
-    for o in order:
-        to = (z + o) % NZ
-        remote(zsend.at[to], zin.at[o], send_sem.at[7], z_sem.at[0], dev(to, x, c, y))
     zin[0] = zsend[z]
 
     @pl.when(c == 1)
@@ -434,10 +444,17 @@
     def _():
         drain(opt_all.at[pl.ds(0, 8)], opt_sem.at[1])
 
-    states = []
+    pieces = []
     for a in range(3):
         table = opt_all[:, c, a].reshape(512, 128)
-        states.append(jnp.dot(onehot[...], table, precision=HIGH, preferred_element_type=F32))
+        for _ in range(3):
+            pieces.append(table.astype(BF16))
+            table = table - pieces[-1].astype(F32)
+    spread = jnp.dot(
+        onehot[...], jnp.concatenate(pieces, axis=1), preferred_element_type=F32
+    )
+    thirds = [spread[:, 128 * i : 128 * i + 128] for i in range(9)]
+    states = [thirds[3 * a] + thirds[3 * a + 1] + thirds[3 * a + 2] for a in range(3)]
     drain(squares.at[pl.ds(0, 31)], norm_sem.at[0])
     squares_total = jnp.sum(jnp.sum(squares[...], axis=0), keepdims=True)
     limit = jnp.float32(1024.0)
@@ -627,7 +644,7 @@
             pltpu.VMEM((4, 2, 3, 4, 128), F32),
             pltpu.VMEM((8, 2, 3, 4, 128), F32),
             pltpu.VMEM((NZ, 2, 3, 32, 128), F32),
-            pltpu.VMEM((256, 512), F32),
+            pltpu.VMEM((256, 512), BF16),
             pltpu.VMEM((4, 4, 4, 64, 128), BF16),
             dma((8,)),
             dma((4, 4)),

time: 71.1 us -> 70.5 us (level)
  no operation moved by 1% of the time
where the time goes in v7:
time: 70.5 us; the launch traced here: 70.4 us
  Pallas kernels  69.1 us (98%)
  between operations  1.29 us (2%)
    pallas_call x1, Pallas kernels, local_step(): pl.pallas_call(reduce_kernel, out_shape=(jax.ShapeDtypeStruct((2, 4, 4, 4...  66.2 us
    pallas_call x1, Pallas kernels, local_step(): pl.pallas_call(result_kernel, out_shape=(jax.ShapeDtypeStruct((1024, 1024...  2.85 us

profile of v7, /device:TPU:1, one launch (start us, length us, event | category | flops | bytes accessed | tf_op | source)
XLA Modules:
  0.0 70.4 jit_solution(14715927013453076398)
XLA Ops:
  1.3 66.2 %adam_reduce.1 = (bf16[2,4,4,4,64,128]{5,4,3,2,1,0:T(8,128)(2,1)}, f32[10,4,128]{2,1,0:T(4,128)}) custom-call(bf16[1024,1024]{1,0:T(8,128)(2,1)} %bitcast.2, s32[1,256]{1,0:T(1,128)} %bitcast.3, s32[1]{0:T(128)S(6)} %copy.10.step_ref, f32[1,4,1024]{2,1,0:T(4,128)} %master_hbm.3, f32[1,4,1024]{2,1,0:T(4,128)} %first_hbm.3, f32[1,4,1024]{2,1,0:T(4,128)} %second_hbm.3), custom_call_target="tpu_custom_call" | custom-call | tf_op jit(solution)/shard_map/adam_reduce/pallas_call | solution.py:617
  67.5 2.8 %adam_results.1 = (bf16[1024,1024]{1,0:T(8,128)(2,1)}, f32[1,4,1024]{2,1,0:T(4,128)}, f32[1,4,1024]{2,1,0:T(4,128)}, f32[1,4,1024]{2,1,0:T(4,128)}) custom-call(bf16[2,4,4,4,64,128]{5,4,3,2,1,0:T(8,128)(2,1)} %get-tuple-element.6.w_all, f32[10,4,128]{2,1,0:T(4,128)} %get-tuple-element.7.small_hbm, s32[1]{0:T(128)S(6)} %copy.10.step_ref, ...), custom_call_target="tpu_custom_call" | custom-call | tf_op jit(solution)/shard_map/adam_results/pallas_call | solution.py:675

commit v8 on v7

--- a/solution.py
+++ b/solution.py
@@ -464,9 +464,9 @@
     def forward(f, j):
         along_x, p, qq, c1, c2, peer1, peer2 = flows[f]
         piece = w_part.at[f, c1, j]
-        remote(piece, piece, send_sem.at[13], ag1_sem.at[f, 2], peer1(flip2(c1)))
         remote(piece, piece, send_sem.at[13], ag1_sem.at[f, 0], peer1(qq))
         remote(piece, piece, send_sem.at[13], ag1_sem.at[f, 1], peer1(p))
+        remote(piece, piece, send_sem.at[13], ag1_sem.at[f, 2], peer1(flip2(c1)))
 
     ag2 = {}
     for f in FLOWS:

time: 70.5 us -> 70.5 us (level)
  no operation moved by 1% of the time
where the time goes in v8:
time: 70.5 us; the launch traced here: 70.3 us
  Pallas kernels  69 us (98%)
  between operations  1.29 us (2%)
    pallas_call x1, Pallas kernels, local_step(): pl.pallas_call(reduce_kernel, out_shape=(jax.ShapeDtypeStruct((2, 4, 4, 4...  66.2 us
    pallas_call x1, Pallas kernels, local_step(): pl.pallas_call(result_kernel, out_shape=(jax.ShapeDtypeStruct((1024, 1024...  2.85 us

profile of v8, /device:TPU:1, one launch (start us, length us, event | category | flops | bytes accessed | tf_op | source)
XLA Modules:
  0.0 70.3 jit_solution(11249620857074453137)
XLA Ops:
  1.3 66.2 %adam_reduce.1 = (bf16[2,4,4,4,64,128]{5,4,3,2,1,0:T(8,128)(2,1)}, f32[10,4,128]{2,1,0:T(4,128)}) custom-call(bf16[1024,1024]{1,0:T(8,128)(2,1)} %bitcast.2, s32[1,256]{1,0:T(1,128)} %bitcast.3, s32[1]{0:T(128)S(6)} %copy.10.step_ref, f32[1,4,1024]{2,1,0:T(4,128)} %master_hbm.3, f32[1,4,1024]{2,1,0:T(4,128)} %first_hbm.3, f32[1,4,1024]{2,1,0:T(4,128)} %second_hbm.3), custom_call_target="tpu_custom_call" | custom-call | tf_op jit(solution)/shard_map/adam_reduce/pallas_call | solution.py:617
  67.4 2.8 %adam_results.1 = (bf16[1024,1024]{1,0:T(8,128)(2,1)}, f32[1,4,1024]{2,1,0:T(4,128)}, f32[1,4,1024]{2,1,0:T(4,128)}, f32[1,4,1024]{2,1,0:T(4,128)}) custom-call(bf16[2,4,4,4,64,128]{5,4,3,2,1,0:T(8,128)(2,1)} %get-tuple-element.6.w_all, f32[10,4,128]{2,1,0:T(4,128)} %get-tuple-element.7.small_hbm, s32[1]{0:T(128)S(6)} %copy.10.step_ref, ...), custom_call_target="tpu_custom_call" | custom-call | tf_op jit(solution)/shard_map/adam_results/pallas_call | solution.py:675

commit v9 on v8

--- a/solution.py
+++ b/solution.py
@@ -473,7 +473,7 @@
         along_x, p, qq, c1, c2, peer1, peer2 = flows[f]
         w_part[f, c1, c2] = rounded[64 * f : 64 * f + 64]
         own = w_part.at[f, c1, c2]
-        for o in (2, 1, 3):
+        for o in (1, 3, 2):
             ag2[f, o] = remote(
                 own, own, send_sem.at[12], ag2_sem.at[f, o - 1], peer2((c2 + o) % 4)
             )

time: 70.5 us -> 70.2 us (level)
  no operation moved by 1% of the time
where the time goes in v9:
time: 70.2 us; the launch traced here: 70 us
  Pallas kernels  68.8 us (98%)
  between operations  1.29 us (2%)
    pallas_call x1, Pallas kernels, local_step(): pl.pallas_call(reduce_kernel, out_shape=(jax.ShapeDtypeStruct((2, 4, 4, 4...  65.9 us
    pallas_call x1, Pallas kernels, local_step(): pl.pallas_call(result_kernel, out_shape=(jax.ShapeDtypeStruct((1024, 1024...  2.85 us

profile of v9, /device:TPU:1, one launch (start us, length us, event | category | flops | bytes accessed | tf_op | source)
XLA Modules:
  0.0 70.0 jit_solution(8365669173297298188)
XLA Ops:
  1.3 65.9 %adam_reduce.1 = (bf16[2,4,4,4,64,128]{5,4,3,2,1,0:T(8,128)(2,1)}, f32[10,4,128]{2,1,0:T(4,128)}) custom-call(bf16[1024,1024]{1,0:T(8,128)(2,1)} %bitcast.2, s32[1,256]{1,0:T(1,128)} %bitcast.3, s32[1]{0:T(128)S(6)} %copy.10.step_ref, f32[1,4,1024]{2,1,0:T(4,128)} %master_hbm.3, f32[1,4,1024]{2,1,0:T(4,128)} %first_hbm.3, f32[1,4,1024]{2,1,0:T(4,128)} %second_hbm.3), custom_call_target="tpu_custom_call" | custom-call | tf_op jit(solution)/shard_map/adam_reduce/pallas_call | solution.py:617
  67.2 2.8 %adam_results.1 = (bf16[1024,1024]{1,0:T(8,128)(2,1)}, f32[1,4,1024]{2,1,0:T(4,128)}, f32[1,4,1024]{2,1,0:T(4,128)}, f32[1,4,1024]{2,1,0:T(4,128)}) custom-call(bf16[2,4,4,4,64,128]{5,4,3,2,1,0:T(8,128)(2,1)} %get-tuple-element.6.w_all, f32[10,4,128]{2,1,0:T(4,128)} %get-tuple-element.7.small_hbm, s32[1]{0:T(128)S(6)} %copy.10.step_ref, ...), custom_call_target="tpu_custom_call" | custom-call | tf_op jit(solution)/shard_map/adam_results/pallas_call | solution.py:675
